TPU v7x, 32 devices: a whole 2x2x4 slice. The times are simulated.
32 devices in a mesh: dp: 8 (over z, y), tensor: 4 (over x, core).
Axes of the slice: x: 2, y: 2, z: 4, core: 2. Of those that a mesh axis runs over, the one named last changes fastest.
Arguments:
- tokens: bfloat16 [16384, 768], P(('dp', 'tensor'))
- first_values: bfloat16 [16384, 384], P(('dp', 'tensor')), may hold values from -6 to 6
- pieces: int32 [16384], P('dp'), may hold values from 0 to 64, as said below
- lengths: int32 [8], P('dp'), may hold values from 256 to 2048, as said below
- w_query: bfloat16 [768, 768], P('dp', 'tensor'), may hold values from -0.21875 to 0.21875
- w_key: bfloat16 [768, 768], P('dp', 'tensor'), may hold values from -0.21875 to 0.21875
- w_value: bfloat16 [768, 384], P('dp'), may hold values from -0.21875 to 0.21875
- w_out: bfloat16 [768, 768], P('tensor', 'dp'), may hold values from -2.5 to 2.5
- w_up: bfloat16 [768, 3072], P('dp', 'tensor'), may hold values from -0.21875 to 0.21875
- w_down: bfloat16 [3072, 768], P('tensor', 'dp'), may hold values from -0.15625 to 0.15625
- gain_attn: float32 [768], replicated, may hold values from 0.1 to 1.9
- gain_mlp: float32 [768], replicated, may hold values from 0.1 to 1.9
- cotangent: bfloat16 [16384, 768], P(('dp', 'tensor')), may hold values from -6 to 6
Outputs:
- output: bfloat16 [16384, 768], P(('dp', 'tensor'))
- d_tokens: float32 [16384, 768], P(('dp', 'tensor'))
- d_first_values: float32 [16384, 384], P(('dp', 'tensor'))
- d_w_query: float32 [768, 768], P('dp', 'tensor')
- d_w_key: float32 [768, 768], P('dp', 'tensor')
- d_w_value: float32 [768, 384], P('dp')
- d_w_out: float32 [768, 768], P('tensor', 'dp')
- d_w_up: float32 [768, 3072], P('dp', 'tensor')
- d_w_down: float32 [3072, 768], P('tensor', 'dp')
- d_gain_attn: float32 [768], replicated
- d_gain_mlp: float32 [768], replicated
- rms: float32 [3], replicated
Inputs may be any that keep to these rules, and one draw needn't show every extreme that they name: `pieces`: each aligned block of 256 tokens carries one number: 0 for text, or a positive number that no other block carries, for a picture piece. `lengths`: 2048 is reached in every draw.
All inputs are finite; a program needn't handle non-finite values.
Results may differ from a plain program's by a relative error of at most 0.018.
Values may be sent and summed in bfloat16 or wider, within the bound.
No kernel may reach another device: no remote copies, remote signals or barrier semaphores. Data moves between devices by JAX's collectives and lax.ppermute only.
A program may use at most 256 MiB of HBM per device.

v0:
```python
import math

import jax
import jax.numpy as jnp
from jax import lax
from jax.experimental import pallas as pl
from jax.experimental.pallas import tpu as pltpu
from jax.sharding import PartitionSpec as P

HD = 64


EPS = 1e-05
NEG = -1e30


def matmul(first_op, second_op):
    return jnp.dot(first_op, second_op, preferred_element_type=jnp.float32)


def matmul_tn(first_op, second_op):
    return lax.dot_general(
        first_op, second_op, (((0,), (0,)), ((), ())), preferred_element_type=jnp.float32
    )


def matmul_nt(first_op, second_op):
    return lax.dot_general(
        first_op, second_op, (((1,), (1,)), ((), ())), preferred_element_type=jnp.float32
    )


def norm_forward(resid, norm_gain):
    centred = resid - jnp.mean(resid, axis=-1, keepdims=True)
    inv_std = lax.rsqrt(jnp.mean(centred * centred, axis=-1, keepdims=True) + EPS)
    normed = centred * inv_std
    return (normed * norm_gain, normed, inv_std)


def norm_backward(upstream, norm_gain, normed, inv_std):
    scaled = upstream * norm_gain
    inner = (
        scaled
        - jnp.mean(scaled, axis=-1, keepdims=True)
        - normed * jnp.mean(scaled * normed, axis=-1, keepdims=True)
    )
    return (inner * inv_std, jnp.sum(upstream * normed, axis=0))


BLK = 256


def nt(a, b):
    return lax.dot_general(a, b, (((1,), (1,)), ((), ())), preferred_element_type=jnp.float32)


def nn(a, b):
    return jnp.dot(a, b, preferred_element_type=jnp.float32)


def diag_allowed(picture):
    key_pos = lax.broadcasted_iota(jnp.int32, (BLK, BLK), 0)
    query_pos = lax.broadcasted_iota(jnp.int32, (BLK, BLK), 1)
    return (key_pos <= query_pos) | (picture > 0)


def pick(table_ref, info_ref, qkv_ref, first_ref, block, kind, head):
    cols = first_ref.shape[2]
    lane = kind * cols + head * HD
    part = qkv_ref[table_ref[block], :, lane : lane + HD]
    if kind == 2:
        other = first_ref[table_ref[block], :, head * HD : (head + 1) * HD]
        part = jnp.where(info_ref[1] > 0, part, other)
    return part


def prepare(table_ref, info_ref, qkv_ref, first_ref, q_aug, k_aug, head):
    blocks, rows = qkv_ref.shape[:2]
    seq = blocks * rows
    for block in range(blocks):
        span = slice(block * rows, (block + 1) * rows)
        part = pick(table_ref, info_ref, qkv_ref, first_ref, block, 0, head)
        q_aug[head, span, :HD] = part * jnp.bfloat16(1.0 / math.sqrt(HD))
        k_aug[head, span, :HD] = pick(table_ref, info_ref, qkv_ref, first_ref, block, 1, head)
    pos = lax.broadcasted_iota(jnp.int32, (seq, HD), 0)
    lane = lax.broadcasted_iota(jnp.int32, (seq, HD), 1)
    bias = jnp.where((lane == 0) & (pos >= info_ref[0]), NEG, 0.0)
    k_aug[head, :, HD:] = bias.astype(k_aug.dtype)
    q_aug[head, :, HD:] = jnp.where(lane == 0, 1.0, 0.0).astype(q_aug.dtype)


def forward_kernel(table_ref, info_ref, qkv_ref, first_ref, out_ref, lse_ref, q_aug, k_aug, v_t, o_t):
    blocks, rows, cols = first_ref.shape
    heads = cols // HD
    seq = blocks * rows
    for head in range(heads):
        prepare(table_ref, info_ref, qkv_ref, first_ref, q_aug, k_aug, head)
        for block in range(blocks):
            part = pick(table_ref, info_ref, qkv_ref, first_ref, block, 2, head)
            v_t[head, :, block * rows : (block + 1) * rows] = part.T

    def per_head(head, carry):
        for block in range(seq // BLK):
            lo, hi = block * BLK, (block + 1) * BLK
            scores = nt(k_aug[head, :hi, :], q_aug[head, lo:hi, :])
            last = jnp.where(diag_allowed(info_ref[2 + block]), scores[lo:], NEG)
            row_max = jnp.max(last, axis=0, keepdims=True)
            if block:
                row_max = jnp.maximum(row_max, jnp.max(scores[:lo], axis=0, keepdims=True))
            tail = jnp.exp(last - row_max)
            total = jnp.sum(tail, axis=0, keepdims=True)
            acc = nn(v_t[head, :, lo:hi], tail.astype(jnp.bfloat16))
            if block:
                front = jnp.exp(scores[:lo] - row_max)
                total = total + jnp.sum(front, axis=0, keepdims=True)
                acc = acc + nn(v_t[head, :, :lo], front.astype(jnp.bfloat16))
            o_t[head, :, lo:hi] = acc / total
            lse_ref[head, :, lo:hi] = row_max + jnp.log(total)
        return carry

    lax.fori_loop(0, heads, per_head, 0)
    for block in range(blocks):
        part = o_t[:, :, block * rows : (block + 1) * rows].reshape(cols, rows)
        out_ref[table_ref[block]] = part.T.astype(out_ref.dtype)


def attend(qkv, first, table, info):
    blocks, rows, cols = first.shape
    heads = cols // HD
    seq = blocks * rows
    smem = pl.BlockSpec(memory_space=pltpu.SMEM)
    vmem = pl.BlockSpec(memory_space=pltpu.VMEM)
    work = heads * seq * (seq + BLK) // 2
    return pl.pallas_call(
        forward_kernel,
        name="attend",
        out_shape=(
            jax.ShapeDtypeStruct((blocks, rows, cols), jnp.bfloat16),
            jax.ShapeDtypeStruct((heads, 1, seq), jnp.float32),
        ),
        in_specs=[smem, smem, vmem, vmem],
        out_specs=(vmem, vmem),
        scratch_shapes=[
            pltpu.VMEM((heads, seq, 2 * HD), jnp.bfloat16),
            pltpu.VMEM((heads, seq, 2 * HD), jnp.bfloat16),
            pltpu.VMEM((heads, HD, seq), jnp.bfloat16),
            pltpu.VMEM((heads, HD, seq), jnp.float32),
        ],
        compiler_params=pltpu.CompilerParams(vmem_limit_bytes=48 << 20),
        cost_estimate=pl.CostEstimate(
            flops=4 * work * HD * 4, transcendentals=work, bytes_accessed=10 * seq * cols
        ),
    )(table, info, qkv, first)


def backward_kernel(
    table_ref, info_ref, qkv_ref, first_ref, g_ref, o_ref, lse_ref, dqkv_ref, dv_ref,
    q_aug, k_aug, v_rows, g_rows, k_t, dq_t, dk_acc, dv_acc, delta,
):
    blocks, rows, cols = first_ref.shape
    heads = cols // HD
    seq = blocks * rows
    for head in range(heads):
        lane = head * HD
        prepare(table_ref, info_ref, qkv_ref, first_ref, q_aug, k_aug, head)
        for block in range(blocks):
            span = slice(block * rows, (block + 1) * rows)
            v_rows[head, span, :] = pick(table_ref, info_ref, qkv_ref, first_ref, block, 2, head)
            k_t[head, :, span] = pick(table_ref, info_ref, qkv_ref, first_ref, block, 1, head).T
            grads = g_ref[table_ref[block], :, lane : lane + HD]
            outs = o_ref[table_ref[block], :, lane : lane + HD].astype(jnp.float32)
            g_rows[head, span, :] = grads
            products = grads.astype(jnp.float32) * outs
            delta[head, :, span] = jnp.sum(products.T, axis=0, keepdims=True)

    def per_head(head, carry):
        dk_acc[head] = jnp.zeros_like(dk_acc[head])
        dv_acc[head] = jnp.zeros_like(dv_acc[head])
        for block in range(seq // BLK):
            lo, hi = block * BLK, (block + 1) * BLK
            q_block = q_aug[head, lo:hi, :]
            g_block = g_rows[head, lo:hi, :]
            lse = lse_ref[head, :, lo:hi]
            shift = delta[head, :, lo:hi]

            def part(start, stop, diagonal):
                probs = jnp.exp(nt(k_aug[head, start:stop, :], q_block) - lse)
                if diagonal:
                    probs = jnp.where(diag_allowed(info_ref[2 + block]), probs, 0.0)
                grad_probs = nt(v_rows[head, start:stop, :], g_block)
                grad_scores = (probs * (grad_probs - shift)).astype(jnp.bfloat16)
                dv_acc[head, start:stop, :] += nn(probs.astype(jnp.bfloat16), g_block)
                dk_acc[head, start:stop, :] += nn(grad_scores, q_block)[:, :HD]
                return nn(k_t[head, :, start:stop], grad_scores)

            acc = part(lo, hi, True)
            if block:
                acc = acc + part(0, lo, False)
            dq_t[head, :, lo:hi] = acc
        return carry

    lax.fori_loop(0, heads, per_head, 0)
    for block in range(blocks):
        span = slice(block * rows, (block + 1) * rows)
        to = table_ref[block]
        part = dq_t[:, :, span].reshape(cols, rows)
        dqkv_ref[to, :, :cols] = (part.T * (1.0 / math.sqrt(HD))).astype(dqkv_ref.dtype)
        for head in range(heads):
            lane = head * HD
            dqkv_ref[to, :, cols + lane : cols + lane + HD] = dk_acc[head, span, :].astype(dqkv_ref.dtype)
            value = dv_acc[head, span, :].astype(dv_ref.dtype)
            dv_ref[to, :, lane : lane + HD] = value
            kept = jnp.where(info_ref[1] > 0, value, jnp.zeros_like(value))
            dqkv_ref[to, :, 2 * cols + lane : 2 * cols + lane + HD] = kept


def attend_back(qkv, first, grad_heads, heads_out, lse, table, info):
    blocks, rows, cols = first.shape
    heads = cols // HD
    seq = blocks * rows
    smem = pl.BlockSpec(memory_space=pltpu.SMEM)
    vmem = pl.BlockSpec(memory_space=pltpu.VMEM)
    work = heads * seq * (seq + BLK) // 2
    return pl.pallas_call(
        backward_kernel,
        name="attend_back",
        out_shape=(
            jax.ShapeDtypeStruct((blocks, rows, 3 * cols), jnp.bfloat16),
            jax.ShapeDtypeStruct((blocks, rows, cols), jnp.bfloat16),
        ),
        in_specs=[smem, smem] + [vmem] * 5,
        out_specs=(vmem, vmem),
        scratch_shapes=[
            pltpu.VMEM((heads, seq, 2 * HD), jnp.bfloat16),
            pltpu.VMEM((heads, seq, 2 * HD), jnp.bfloat16),
            pltpu.VMEM((heads, seq, HD), jnp.bfloat16),
            pltpu.VMEM((heads, seq, HD), jnp.bfloat16),
            pltpu.VMEM((heads, HD, seq), jnp.bfloat16),
            pltpu.VMEM((heads, HD, seq), jnp.float32),
            pltpu.VMEM((heads, seq, HD), jnp.float32),
            pltpu.VMEM((heads, seq, HD), jnp.float32),
            pltpu.VMEM((heads, 1, seq), jnp.float32),
        ],
        compiler_params=pltpu.CompilerParams(vmem_limit_bytes=56 << 20),
        cost_estimate=pl.CostEstimate(
            flops=10 * work * HD * 4, transcendentals=work, bytes_accessed=24 * seq * cols
        ),
    )(table, info, qkv, first, grad_heads, heads_out, lse)


def gelu_tanh(pre_act):
    return jax.nn.gelu(pre_act, approximate=True)


X_SWAP = [(0, 2), (1, 3), (2, 0), (3, 1)]
CORE_SWAP = [(0, 1), (1, 0), (2, 3), (3, 2)]


def swap_x(v):
    return lax.ppermute(v, "tensor", X_SWAP)


def swap_core(v):
    return lax.ppermute(v, "tensor", CORE_SWAP)


def gather_rel(own):
    from_core = swap_core(own)
    from_x = swap_x(own)
    from_diag = swap_core(from_x)
    return jnp.concatenate([own, from_x, from_core, from_diag], axis=0)


def scatter_rel(parts):
    low = parts.astype(jnp.bfloat16)
    from_core = swap_core(low[2:4]).astype(jnp.float32)
    pair = parts[0:2] + from_core
    from_x = swap_x(pair[1].astype(jnp.bfloat16)).astype(jnp.float32)
    return pair[0] + from_x


def exchange_rel(blocks):
    from_x = swap_x(blocks[jnp.array([1, 3])])
    to_core = jnp.stack([blocks[2], from_x[1]])
    from_core = swap_core(to_core)
    return jnp.stack([blocks[0], from_x[0], from_core[0], from_core[1]])


def body(
    tokens,
    first_values,
    pieces,
    lengths,
    w_query,
    w_key,
    w_value,
    w_out,
    w_up,
    w_down,
    gain_attn,
    gain_mlp,
    cotangent,
):
    dp_size = lax.axis_size("dp")
    rank = lax.axis_index("tensor")
    core = rank % 2
    rows, model_dim = tokens.shape
    seq_len = rows * 4
    cols = w_query.shape[1]
    shard = w_query.shape[0]
    hidden_cols = w_up.shape[1]
    valid_len = lengths[0]
    positions = rank * rows + lax.iota(jnp.int32, rows)
    valid = (positions < valid_len).astype(jnp.float32)[:, None]
    table = (jnp.array([0, 2, 1, 3])[jnp.arange(4) ^ rank]).astype(jnp.int32)
    fresh = (rank < 2).astype(jnp.int32)
    info = jnp.concatenate([valid_len[None], fresh[None], pieces[::BLK]])

    value_cols = lax.dynamic_slice_in_dim(w_value, core * cols, cols, 1)
    early = jnp.concatenate([w_query, w_key, value_cols], axis=1)
    late = jnp.concatenate([w_up, w_down.T, w_out.T], axis=1)
    late_all = lax.all_gather(late, "dp", axis=0, tiled=True)
    early_all = lax.all_to_all(
        jnp.broadcast_to(early[None], (dp_size,) + early.shape), "dp", 0, 0
    ).reshape(model_dim, 3 * cols)

    tokens_wide = tokens.astype(jnp.float32)
    norm_one, normed_one, inv_one = norm_forward(tokens_wide, gain_attn)
    attn_input = norm_one.astype(jnp.bfloat16)
    input_rel = gather_rel(attn_input)
    first_x = lax.ppermute(first_values, "tensor", [(0, 2), (1, 3)])
    first_two = jnp.stack([first_values, first_x])
    first_mine = lax.dynamic_slice_in_dim(first_two, core * cols, cols, 2)
    first_other = lax.dynamic_slice_in_dim(first_two, (1 - core) * cols, cols, 2)
    first_rel = jnp.concatenate([first_mine, swap_core(first_other)], axis=0)
    cot_rel = gather_rel(cotangent)

    qkv = matmul(input_rel, early_all).astype(jnp.bfloat16).reshape(4, rows, 3 * cols)
    heads_rel, log_sums = attend(qkv, first_rel, table, info)
    heads_mine = exchange_rel(heads_rel)
    heads_cat = jnp.concatenate([heads_mine[i] for i in range(4)], axis=1)

    out_own = late_all[:, 2 * hidden_cols :]
    out_x = swap_x(out_own)
    out_pair = jnp.concatenate([out_own, out_x], axis=1)
    out_all = jnp.concatenate([out_pair, swap_core(out_pair)], axis=1)
    attn_out = matmul_nt(heads_cat, out_all)
    resid_mid = tokens_wide + attn_out
    norm_two, normed_two, inv_two = norm_forward(resid_mid, gain_mlp)
    mlp_input = norm_two.astype(jnp.bfloat16)
    mlp_rel = gather_rel(mlp_input)
    up_w = late_all[:, :hidden_cols]
    down_t = late_all[:, hidden_cols : 2 * hidden_cols]
    up_pre = matmul(mlp_rel, up_w)
    hidden_act, gelu_pull = jax.vjp(gelu_tanh, up_pre)
    hidden = hidden_act.astype(jnp.bfloat16)
    grad_hidden = matmul(cot_rel, down_t)
    grad_up_pre = gelu_pull(grad_hidden)[0].astype(jnp.bfloat16)
    grad_mlp_input = scatter_rel(matmul_nt(grad_up_pre, up_w).reshape(4, rows, model_dim))
    mlp_out = scatter_rel(matmul_nt(hidden, down_t).reshape(4, rows, model_dim))
    final = resid_mid + mlp_out
    squares = jnp.stack(
        [
            jnp.sum(valid * final * final),
            jnp.sum(valid * attn_out * attn_out),
            jnp.sum(valid * mlp_out * mlp_out),
            jnp.sum(valid),
        ]
    )
    grad_down_t = matmul_tn(cot_rel, hidden).astype(jnp.bfloat16)
    grad_up_w = matmul_tn(mlp_rel, grad_up_pre).astype(jnp.bfloat16)
    mlp_share = lax.psum_scatter(
        jnp.concatenate([grad_up_w, grad_down_t], axis=1), "dp", scatter_dimension=0, tiled=True
    ).astype(jnp.float32)

    out_grad = cotangent.astype(jnp.float32)
    grad_two, gain_two_grad = norm_backward(grad_mlp_input, gain_mlp, normed_two, inv_two)
    resid_grad = out_grad + grad_two
    resid_low = resid_grad.astype(jnp.bfloat16)
    grad_heads = matmul(resid_low, out_all).astype(jnp.bfloat16)
    grad_heads_rel = exchange_rel(grad_heads.reshape(rows, 4, cols).transpose(1, 0, 2))
    grad_out_rel = matmul_tn(resid_low, heads_cat).reshape(model_dim, 4, cols)
    grad_out_t = scatter_rel(grad_out_rel.transpose(1, 0, 2))

    grad_qkv, grad_v_rel = attend_back(
        qkv, first_rel, grad_heads_rel, heads_rel, log_sums, table, info
    )
    grad_qkv = grad_qkv.reshape(seq_len, 3 * cols)
    grad_qkv_w = matmul_tn(input_rel, grad_qkv)
    grad_attn_input = scatter_rel(matmul_nt(grad_qkv, early_all).reshape(4, rows, model_dim))
    first_from_x = lax.ppermute(
        grad_v_rel[jnp.array([1, 3])], "tensor", [(2, 0), (3, 1)]
    )
    first_here = jnp.where(rank < 2, first_from_x, grad_v_rel[jnp.array([0, 2])])
    first_mine = first_here[0]
    first_peer = swap_core(first_here[1])
    first_grad = jnp.where(
        core == 0,
        jnp.concatenate([first_mine, first_peer], axis=1),
        jnp.concatenate([first_peer, first_mine], axis=1),
    ).astype(jnp.float32)
    grad_one, gain_one_grad = norm_backward(grad_attn_input, gain_attn, normed_one, inv_one)
    token_grad = resid_grad + grad_one

    tail_parts = jnp.concatenate([grad_qkv_w, grad_out_t], axis=1).astype(jnp.bfloat16)
    tail_all = lax.all_to_all(tail_parts.reshape(dp_size, shard, 4 * cols), "dp", 0, 0)
    tail_share = jnp.sum(tail_all.astype(jnp.float32), axis=0)
    value_own = tail_share[:, 2 * cols : 3 * cols]
    value_x = lax.ppermute(value_own, "tensor", [(0, 2), (1, 3)])
    value_here = jnp.where(rank < 2, value_own, value_x)
    value_peer = swap_core(value_here)
    value_share = jnp.where(
        core == 0,
        jnp.concatenate([value_here, value_peer], axis=1),
        jnp.concatenate([value_peer, value_here], axis=1),
    )
    small = jnp.concatenate([gain_one_grad, gain_two_grad, squares])
    count = dp_size * 4
    small_all = lax.all_to_all(
        jnp.broadcast_to(small[None], (count,) + small.shape), ("dp", "tensor"), 0, 0
    )
    total = jnp.sum(small_all, axis=0)
    square_total = total[2 * model_dim :]
    rms = jnp.sqrt(square_total[:3] / (square_total[3] * model_dim))
    return (
        final.astype(jnp.bfloat16),
        token_grad,
        first_grad,
        tail_share[:, :cols],
        tail_share[:, cols : 2 * cols],
        value_share,
        tail_share[:, 3 * cols :].T,
        mlp_share[:, :hidden_cols],
        mlp_share[:, hidden_cols:].T,
        total[:model_dim],
        total[model_dim : 2 * model_dim],
        rms,
    )


def solution(mesh):
    in_specs = (
        P(("dp", "tensor"), None),
        P(("dp", "tensor"), None),
        P("dp"),
        P("dp"),
        P("dp", "tensor"),
        P("dp", "tensor"),
        P("dp", None),
        P("tensor", "dp"),
        P("dp", "tensor"),
        P("tensor", "dp"),
        P(),
        P(),
        P(("dp", "tensor"), None),
    )
    out_specs = (
        P(("dp", "tensor"), None),
        P(("dp", "tensor"), None),
        P(("dp", "tensor"), None),
        P("dp", "tensor"),
        P("dp", "tensor"),
        P("dp", None),
        P("tensor", "dp"),
        P("dp", "tensor"),
        P("tensor", "dp"),
        P(),
        P(),
        P(),
    )
    return jax.shard_map(body, mesh=mesh, in_specs=in_specs, out_specs=out_specs, check_vma=False)
```

profile of v0, /device:TPU:0, one launch (start us, length us, event | category | flops | bytes accessed | tf_op | source)
XLA Modules:
  0.0 399.0 jit_solution(7488289610869360962)
XLA Ops:
  13.2 3.0 collective-permute-start
  17.5 5.8 %all-to-all-start = ((bf16[8,96,576]{2,1,0:T(8,128)(2,1)}), bf16[8,96,576]{2,1,0:T(8,128)(2,1)S(1)}, u32[]{:S(2)}, u32[]{:S(2)}) async-start(bf16[8,96,576]{2,1,0:T(8,128)(2,1)} %broadcast_in_dim.19), calls=%async_computation | async-start | bytes 1966080 | tf_op jit(solution)/shard_map/all_to_all | solution.py:323
  23.4 2.5 collective-permute-start.3
  25.9 8.2 %collective-permute-done = bf16[512,768]{1,0:T(8,128)(2,1)} collective-permute-done((bf16[512,768]{1,0:T(8,128)(2,1)S(1)}, bf16[512,768]{1,0:T(8,128)(2,1)}, u32[]{:S(2)}, u32[]{:S(2)}) %collective-permute-start) | collective-permute-done | bytes 786464 | tf_op jit(solution)/shard_map/ppermute | solution.py:260
  35.6 5.8 %collective-permute-done.3 = bf16[512,384]{1,0:T(8,128)(2,1)S(1)} collective-permute-done((bf16[512,384]{1,0:T(8,128)(2,1)S(1)}, bf16[512,384]{1,0:T(8,128)(2,1)S(1)}, u32[]{:S(2)}, u32[]{:S(2)}) %collective-permute-start.3) | collective-permute-done | bytes 393248 | tf_op jit(solution)/shard_map/ppermute | solution.py:331
  42.2 2.5 fusion.44
  47.0 2.3 pad_maximum_fusion.5.first_ref
  49.3 7.8 %all-to-all-done = bf16[8,96,576]{2,1,0:T(8,128)(2,1)S(1)} async-done(((bf16[8,96,576]{2,1,0:T(8,128)(2,1)}), bf16[8,96,576]{2,1,0:T(8,128)(2,1)S(1)}, u32[]{:S(2)}, u32[]{:S(2)}) %all-to-all-start) | async-done | bytes 884768 | tf_op jit(solution)/shard_map/all_to_all | solution.py:323
  58.0 5.1 %convolution_convert_fusion = bf16[2048,576]{0,1:T(8,128)(2,1)} fusion(bf16[768,576]{1,0:T(8,128)(2,1)S(1)} %bitcast.125, bf16[512,768]{1,0:T(8,128)(2,1)} %collective-permute-done.2, bf16[512,768]{1,0:T(8,128)(2,1)} %collective-permute-done.1, bf16[512,768]{1,0:T(8,128)(2,1)} %collective-permute-done, bf16[512,768]{1,0:T(8,128)(2,1)S(1)} %fusion.13), kind=kOutput, calls=%fused_computation.23 | convolution fusion | flops 1825701888 | bytes 6389760 | tf_op jit(solution)/shard_map/dot_general | solution.py:18
  63.1 3.3 copy.72
  68.4 22.7 %attend.1 = (bf16[4,512,192]{2,1,0:T(8,128)(2,1)S(1)}, f32[3,1,2048]{2,1,0:T(1,128)S(1)}) custom-call(s32[4]{0:T(128)S(1)} %gather_fusion, s32[10]{0:T(128)S(1)} %pad_add_fusion.info_ref, bf16[4,512,576]{2,1,0:T(8,128)(2,1)S(1)} %bitcast.111, bf16[4,512,192]{2,1,0:T(8,128)(2,1)S(1)} %copy-done.3), custom_call_target="tpu_custom_call" | custom-call | flops 7247757312 | bytes 3932160 | tf_op jit(solution)/shard_map/attend/pallas_call | solution.py:134
  98.3 10.5 %collective-permute-done.5 = bf16[2,512,192]{2,1,0:T(8,128)(2,1)S(1)} collective-permute-done((bf16[2,512,192]{2,1,0:T(8,128)(2,1)S(1)}, bf16[2,512,192]{2,1,0:T(8,128)(2,1)S(1)}, u32[]{:S(2)}, u32[]{:S(2)}) %collective-permute-start.5) | collective-permute-done | bytes 393248 | tf_op jit(solution)/shard_map/ppermute | solution.py:260
  109.1 6.9 %collective-permute-done.7 = bf16[768,192]{1,0:T(8,128)(2,1)S(1)} collective-permute-done((bf16[768,192]{1,0:T(8,128)(2,1)S(1)}, bf16[768,192]{1,0:T(8,128)(2,1)S(1)}, u32[]{:S(2)}, u32[]{:S(2)}) %collective-permute-start.7) | collective-permute-done | bytes 294944 | tf_op jit(solution)/shard_map/ppermute | solution.py:260
  118.3 2.2 fusion.62
  123.4 13.6 %collective-permute-done.14 = bf16[512,768]{1,0:T(8,128)(2,1)} collective-permute-done((bf16[512,768]{1,0:T(8,128)(2,1)}, bf16[512,768]{1,0:T(8,128)(2,1)}, u32[]{:S(2)}, u32[]{:S(2)}) %collective-permute-start.14) | collective-permute-done | bytes 786464 | tf_op jit(solution)/shard_map/ppermute | solution.py:260
  139.6 13.8 %collective-permute-done.9 = bf16[512,768]{1,0:T(8,128)(2,1)} collective-permute-done((bf16[512,768]{1,0:T(8,128)(2,1)}, bf16[512,768]{1,0:T(8,128)(2,1)}, u32[]{:S(2)}, u32[]{:S(2)}) %collective-permute-start.9) | collective-permute-done | bytes 786464 | tf_op jit(solution)/shard_map/ppermute | solution.py:260
  157.6 3.1 fusion.42
  160.6 5.1 %copy.76 = bf16[768,2048]{1,0:T(8,128)(2,1)} copy(bf16[768,2048]{0,1:T(8,128)(2,1)} %fusion.42) | data formatting | bytes 6291456 | tf_op jit(solution)/shard_map/dot_general | solution.py:22
  167.8 5.1 %fusion.34 = f32[2048,768]{1,0:T(8,128)S(1)} fusion(bf16[768,1728]{1,0:T(8,128)(2,1)} %all-gather.2.cloned.1.call-done, bf16[512,768]{1,0:T(8,128)(2,1)} %collective-permute-done.11, bf16[512,768]{1,0:T(8,128)(2,1)} %collective-permute-done.10, bf16[512,768]{1,0:T(8,128)(2,1)} %collective-permute-done.9, bf16[512,768]{1,0:T(8,128)(2,1)} %multiply_convert_fusion.1), kind=kOutput, calls=%fused_computation.81 | convolution fusion | flops 2428502016 | bytes 10616832 | tf_op jit(solution)/shard_map/dot_general | solution.py:18
  172.9 3.9 fusion.28
  177.5 9.2 %fusion.6 = bf16[2048,768]{1,0:T(8,128)(2,1)S(1)} fusion(f32[2048,768]{1,0:T(8,128)S(1)} %fusion.34, bf16[2048,768]{1,0:T(8,128)(2,1)} %constant_dynamic-update-slice_fusion, bf16[768,1728]{1,0:T(8,128)(2,1)S(1)} %copy-done.35), kind=kOutput, calls=%fused_computation.13 | convolution fusion | flops 2447376384 | bytes 13762560 | tf_op jit(solution)/shard_map/dot_general | solution.py:18
  186.7 2.7 fusion.32
  189.5 2.5 copy-done.15
  192.6 5.7 %convolution_convert_fusion.1 = bf16[768,768]{0,1:T(8,128)(2,1)S(1)} fusion(bf16[2048,768]{1,0:T(8,128)(2,1)} %constant_dynamic-update-slice_fusion, f32[2048,768]{1,0:T(8,128)S(1)} %fusion.34), kind=kOutput, calls=%fused_computation.62 | convolution fusion | flops 2430664704 | bytes 10616832 | tf_op jit(solution)/shard_map/dot_general | solution.py:22
  205.8 4.6 %convolution_convert_fusion.2 = bf16[768,768]{0,1:T(8,128)(2,1)S(1)} fusion(bf16[2048,768]{1,0:T(8,128)(2,1)S(1)} %fusion.6, bf16[512,768]{1,0:T(8,128)(2,1)} %collective-permute-done.11, bf16[512,768]{1,0:T(8,128)(2,1)} %collective-permute-done.10, bf16[512,768]{1,0:T(8,128)(2,1)} %collective-permute-done.9, bf16[512,768]{1,0:T(8,128)(2,1)} %multiply_convert_fusion.1), kind=kOutput, calls=%fused_computation.63 | convolution fusion | flops 2429091840 | bytes 7471104 | tf_op jit(solution)/shard_map/dot_general | solution.py:22
  211.9 4.3 %copy.85 = bf16[768,1536]{1,0:T(8,128)(2,1)} copy(bf16[768,1536]{0,1:T(8,128)(2,1)} %pad_maximum_fusion.2) | data formatting | bytes 4718592
  216.2 4.2 %collective-permute-done.13 = bf16[512,768]{1,0:T(8,128)(2,1)} collective-permute-done((bf16[512,768]{1,0:T(8,128)(2,1)}, bf16[512,768]{1,0:T(8,128)(2,1)}, u32[]{:S(2)}, u32[]{:S(2)}) %collective-permute-start.13) | collective-permute-done | bytes 786464 | tf_op jit(solution)/shard_map/ppermute | solution.py:260
  220.4 15.7 %collective-permute-done.18 = bf16[512,768]{1,0:T(8,128)(2,1)S(1)} collective-permute-done((bf16[512,768]{1,0:T(8,128)(2,1)}, bf16[512,768]{1,0:T(8,128)(2,1)S(1)}, u32[]{:S(2)}, u32[]{:S(2)}) %collective-permute-start.18) | collective-permute-done | bytes 786464 | tf_op jit(solution)/shard_map/ppermute | solution.py:260
  236.1 5.0 %fusion.22 = (f32[]{:T(128)}, f32[]{:T(128)}, f32[512]{0:T(512)S(1)}, f32[512]{0:T(512)S(1)}, f32[768]{0:T(1024)S(1)}, /*index=5*/f32[]{:T(128)}, bf16[512,768]{1,0:T(8,128)(2,1)}) fusion(bf16[512,768]{1,0:T(8,128)(2,1)} %collective-permute-done.13, f32[2,512,768]{2,1,0:T(8,128)} %copy-done.17, f32[512]{0:T(512)S(1)} %fusion.52, ...), kind=kLoop, calls=%fused_computation.47 | loop fusion | flops 9042173 | bytes 8667148 | tf_op jit(solution)/shard_map/reduce_sum | solution.py:366
  250.8 2.5 fusion.46
  253.5 9.1 %collective-permute-done.19 = bf16[2,512,192]{2,1,0:T(8,128)(2,1)S(1)} collective-permute-done((bf16[2,512,192]{2,1,0:T(8,128)(2,1)}, bf16[2,512,192]{2,1,0:T(8,128)(2,1)S(1)}, u32[]{:S(2)}, u32[]{:S(2)}) %collective-permute-start.19) | collective-permute-done | bytes 393248 | tf_op jit(solution)/shard_map/ppermute | solution.py:260
  265.9 32.3 %attend_back.1 = (bf16[4,512,576]{2,1,0:T(8,128)(2,1)}, bf16[4,512,192]{2,1,0:T(8,128)(2,1)}) custom-call(s32[4]{0:T(128)} %copy-done.6, s32[10]{0:T(128)} %copy-done.5, bf16[4,512,576]{2,1,0:T(8,128)(2,1)} %bitcast.112, bf16[4,512,192]{2,1,0:T(8,128)(2,1)} %pad_maximum_fusion.5.first_ref, bf16[4,512,192]{2,1,0:T(8,128)(2,1)} %pad_maximum_fusion.6.g_ref, ...), custom_call_target="tpu_custom_call" | custom-call | flops 18119393280 | bytes 9437184 | tf_op jit(solution)/shard_map/attend_back/pallas_call | solution.py:224
  298.2 4.6 %fusion.66 = f32[2048,768]{1,0:T(8,128)S(1)} fusion(bf16[2048,576]{1,0:T(8,128)(2,1)} %bitcast.131, bf16[768,576]{1,0:T(8,128)(2,1)S(1)} %bitcast.126), kind=kOutput, calls=%fused_computation.158 | convolution fusion | flops 1811939328 | bytes 9535488 | tf_op jit(solution)/shard_map/dot_general | solution.py:28
  304.2 2.7 copy-done.21
  306.9 3.7 convolution_convert_fusion.3
  310.8 2.5 pad_maximum_fusion.4
  313.3 4.4 %all-to-all-start.1 = ((bf16[8,96,768]{2,1,0:T(8,128)(2,1)}), bf16[8,96,768]{2,1,0:T(8,128)(2,1)}, u32[]{:S(2)}, u32[]{:S(2)}) async-start(bf16[8,96,768]{2,1,0:T(8,128)(2,1)} %pad_maximum_fusion.4), calls=%async_computation.1 | async-start | bytes 2359296 | tf_op jit(solution)/shard_map/all_to_all | solution.py:406
  321.1 3.8 slice.231
  326.7 8.5 %collective-permute-done.23 = bf16[2,512,192]{2,1,0:T(8,128)(2,1)S(1)} collective-permute-done((bf16[2,512,192]{2,1,0:T(8,128)(2,1)}, bf16[2,512,192]{2,1,0:T(8,128)(2,1)S(1)}, u32[]{:S(2)}, u32[]{:S(2)}) %collective-permute-start.23) | collective-permute-done | bytes 393248 | tf_op jit(solution)/shard_map/ppermute | solution.py:391
  336.0 2.7 convert_add_fusion
  341.2 5.7 %all-to-all-done.1 = bf16[8,96,768]{2,1,0:T(8,128)(2,1)} async-done(((bf16[8,96,768]{2,1,0:T(8,128)(2,1)}), bf16[8,96,768]{2,1,0:T(8,128)(2,1)}, u32[]{:S(2)}, u32[]{:S(2)}) %all-to-all-start.1) | async-done | bytes 1179680 | tf_op jit(solution)/shard_map/all_to_all | solution.py:406
  349.0 3.3 collective-permute-start.27
  354.7 6.6 %collective-permute-done.27 = f32[96,192]{1,0:T(8,128)S(1)} collective-permute-done((f32[96,192]{1,0:T(8,128)}, f32[96,192]{1,0:T(8,128)S(1)}, u32[]{:S(2)}, u32[]{:S(2)}) %collective-permute-start.27) | collective-permute-done | bytes 73760 | tf_op jit(solution)/shard_map/ppermute | solution.py:409
  367.2 2.5 fusion.18
  369.8 2.6 concatenate.73
  373.2 6.6 %all-to-all-start.2 = ((f32[32,1,1540]{2,1,0:T(1,128)}), f32[32,1,1540]{2,1,0:T(1,128)S(1)}, u32[]{:S(2)}, u32[]{:S(2)}) async-start(f32[32,1,1540]{2,1,0:T(1,128)} %broadcast_in_dim.24), calls=%async_computation.2 | async-start | bytes 425984 | tf_op jit(solution)/shard_map/all_to_all | solution.py:419
  379.8 3.5 fusion.17
  383.3 5.9 %all-to-all-done.2 = f32[32,1,1540]{2,1,0:T(1,128)S(1)} async-done(((f32[32,1,1540]{2,1,0:T(1,128)}), f32[32,1,1540]{2,1,0:T(1,128)S(1)}, u32[]{:S(2)}, u32[]{:S(2)}) %all-to-all-start.2) | async-done | bytes 197152 | tf_op jit(solution)/shard_map/all_to_all | solution.py:419
  (226 shorter events, 82.1 us)
Async XLA Ops:
  7.2 89.3 %all-gather.2.cloned.1.call-start = ((), (), s32[]{:S(2)}) async-start(), calls=%async_computation.4 | async-start | bytes 3096576 | tf_op jit(solution)/shard_map/all_gather | solution.py:322
  13.2 43.8 %copy-start.19 = (bf16[512,768]{1,0:T(8,128)(2,1)}, bf16[512,768]{1,0:T(8,128)(2,1)S(1)}, u32[]{:S(2)}) copy-start(bf16[512,768]{1,0:T(8,128)(2,1)S(1)} %fusion.13) | copy-start | bytes 2359300
  13.2 21.0 %collective-permute-start = (bf16[512,768]{1,0:T(8,128)(2,1)S(1)}, bf16[512,768]{1,0:T(8,128)(2,1)}, u32[]{:S(2)}, u32[]{:S(2)}) collective-permute-start(bf16[512,768]{1,0:T(8,128)(2,1)S(1)} %fusion.13), channel_id=1, source_target_pairs={{0,2},{1,3},{2,0},{3,1},{4,6},{5,7},{6,4},{7,5},{8,10},{9,11},{10,... | collective-permute-start | bytes 2359304 | tf_op jit(solution)/shard_map/ppermute | solution.py:260
  16.3 28.4 %copy-start.8 = (s32[4]{0:T(128)S(1)}, s32[4]{0:T(128)}, u32[]{:S(2)}) copy-start(s32[4]{0:T(128)} %constant.66.clone) | copy-start | bytes 52
  16.4 29.0 %copy-start.42 = (s32[2]{0:T(128)S(1)}, s32[2]{0:T(128)}, u32[]{:S(2)}) copy-start(s32[2]{0:T(128)} %constant.74) | copy-start | bytes 28
  17.5 39.6 %all-to-all-start = ((bf16[8,96,576]{2,1,0:T(8,128)(2,1)}), bf16[8,96,576]{2,1,0:T(8,128)(2,1)S(1)}, u32[]{:S(2)}, u32[]{:S(2)}) async-start(bf16[8,96,576]{2,1,0:T(8,128)(2,1)} %broadcast_in_dim.19), calls=%async_computation | async-start | bytes 1966080 | tf_op jit(solution)/shard_map/all_to_all | solution.py:323
  23.3 330.2 %reduce-scatter.4.cloned.1.call-start = ((), (), s32[]{:S(2)}) async-start(), calls=%async_computation.5 | async-start | bytes 2654208
  23.4 18.1 %collective-permute-start.3 = (bf16[512,384]{1,0:T(8,128)(2,1)S(1)}, bf16[512,384]{1,0:T(8,128)(2,1)S(1)}, u32[]{:S(2)}, u32[]{:S(2)}) collective-permute-start(bf16[512,384]{1,0:T(8,128)(2,1)S(1)} %copy-done.31), channel_id=1, source_target_pairs={{0,2},{1,3},{4,6},{5,7},{8,10},{9,11},{12,14},{13,15},{16,18},{17,... | collective-permute-start | bytes 1179656 | tf_op jit(solution)/shard_map/ppermute | solution.py:331
  25.8 23.4 %collective-permute-start.1 = (bf16[512,768]{1,0:T(8,128)(2,1)S(1)}, bf16[512,768]{1,0:T(8,128)(2,1)}, u32[]{:S(2)}, u32[]{:S(2)}) collective-permute-start(bf16[512,768]{1,0:T(8,128)(2,1)S(1)} %fusion.13), channel_id=1, source_target_pairs={{0,1},{1,0},{2,3},{3,2},{4,5},{5,4},{6,7},{7,6},{8,9},{9,8},{10,11... | collective-permute-start | bytes 2359304 | tf_op jit(solution)/shard_map/ppermute | solution.py:264
  34.2 22.9 %collective-permute-start.2 = (bf16[512,768]{1,0:T(8,128)(2,1)}, bf16[512,768]{1,0:T(8,128)(2,1)}, u32[]{:S(2)}, u32[]{:S(2)}) collective-permute-start(bf16[512,768]{1,0:T(8,128)(2,1)} %collective-permute-done), channel_id=1, source_target_pairs={{0,1},{1,0},{2,3},{3,2},{4,5},{5,4},{6,7},{7,6},{8,9},{9,8},{10,11... | collective-permute-start | bytes 2359304 | tf_op jit(solution)/shard_map/ppermute | solution.py:264
  44.7 2.3 collective-permute-start.4
  45.4 21.0 %copy-start.6 = (s32[4]{0:T(128)}, s32[4]{0:T(128)S(1)}, u32[]{:S(2)}) copy-start(s32[4]{0:T(128)S(1)} %gather_fusion) | copy-start | bytes 52
  45.5 20.9 %copy-start.5 = (s32[10]{0:T(128)}, s32[10]{0:T(128)S(1)}, u32[]{:S(2)}) copy-start(s32[10]{0:T(128)S(1)} %pad_add_fusion.info_ref) | copy-start | bytes 124
  66.3 24.8 %copy-start.2 = (bf16[2048,576]{1,0:T(8,128)(2,1)}, bf16[2048,576]{1,0:T(8,128)(2,1)S(1)}, u32[]{:S(2)}) copy-start(bf16[2048,576]{1,0:T(8,128)(2,1)S(1)} %copy.72) | copy-start | bytes 7077892
  92.1 24.1 %copy-start.7 = (f32[3,1,2048]{2,1,0:T(1,128)}, f32[3,1,2048]{2,1,0:T(1,128)S(1)}, u32[]{:S(2)}) copy-start(f32[3,1,2048]{2,1,0:T(1,128)S(1)} %get-tuple-element.17.lse_ref) | copy-start | bytes 73732
  93.9 14.9 %collective-permute-start.5 = (bf16[2,512,192]{2,1,0:T(8,128)(2,1)S(1)}, bf16[2,512,192]{2,1,0:T(8,128)(2,1)S(1)}, u32[]{:S(2)}, u32[]{:S(2)}) collective-permute-start(bf16[2,512,192]{2,1,0:T(8,128)(2,1)S(1)} %gather_fusion.1), channel_id=1, source_target_pairs={{0,2},{1,3},{2,0},{3,1},{4,6},{5,7},{6,4},{7,5},{8,10},{9,11},{10,... | collective-permute-start | bytes 1179656 | tf_op jit(solution)/shard_map/ppermute | solution.py:260
  96.5 21.7 %copy-start.24 = (bf16[512,192]{1,0:T(8,128)(2,1)}, bf16[512,192]{1,0:T(8,128)(2,1)S(1)}, u32[]{:S(2)}) copy-start(bf16[512,192]{1,0:T(8,128)(2,1)S(1)} %get-tuple-element.97) | copy-start | bytes 589828
  97.7 22.8 %copy-start.22 = (bf16[768,192]{1,0:T(8,128)(2,1)}, bf16[768,192]{1,0:T(8,128)(2,1)S(1)}, u32[]{:S(2)}) copy-start(bf16[768,192]{1,0:T(8,128)(2,1)S(1)} %slice.216) | copy-start | bytes 884740
  97.7 18.3 %collective-permute-start.7 = (bf16[768,192]{1,0:T(8,128)(2,1)S(1)}, bf16[768,192]{1,0:T(8,128)(2,1)S(1)}, u32[]{:S(2)}, u32[]{:S(2)}) collective-permute-start(bf16[768,192]{1,0:T(8,128)(2,1)S(1)} %slice.216), channel_id=1, source_target_pairs={{0,2},{1,3},{2,0},{3,1},{4,6},{5,7},{6,4},{7,5},{8,10},{9,11},{10,... | collective-permute-start | bytes 884744 | tf_op jit(solution)/shard_map/ppermute | solution.py:260
  109.0 8.8 %collective-permute-start.6 = (bf16[2,512,192]{2,1,0:T(8,128)(2,1)S(1)}, bf16[2,512,192]{2,1,0:T(8,128)(2,1)S(1)}, u32[]{:S(2)}, u32[]{:S(2)}) collective-permute-start(bf16[2,512,192]{2,1,0:T(8,128)(2,1)S(1)} %pad_maximum_fusion.12), channel_id=1, source_target_pairs={{0,1},{1,0},{2,3},{3,2},{4,5},{5,4},{6,7},{7,6},{8,9},{9,8},{10,11... | collective-permute-start | bytes 1179656 | tf_op jit(solution)/shard_map/ppermute | solution.py:264
  116.2 2.1 collective-permute-start.8
  116.3 20.7 %collective-permute-start.14 = (bf16[512,768]{1,0:T(8,128)(2,1)}, bf16[512,768]{1,0:T(8,128)(2,1)}, u32[]{:S(2)}, u32[]{:S(2)}) collective-permute-start(bf16[512,768]{1,0:T(8,128)(2,1)} %param.30), channel_id=1, source_target_pairs={{0,2},{1,3},{2,0},{3,1},{4,6},{5,7},{6,4},{7,5},{8,10},{9,11},{10,... | collective-permute-start | bytes 2359304 | tf_op jit(solution)/shard_map/ppermute | solution.py:260
  122.0 35.6 %copy-start.20 = (bf16[512,768]{1,0:T(8,128)(2,1)S(1)}, bf16[512,768]{1,0:T(8,128)(2,1)}, u32[]{:S(2)}) copy-start(bf16[512,768]{1,0:T(8,128)(2,1)} %copy-done.19) | copy-start | bytes 2359300
  122.0 31.4 %collective-permute-start.9 = (bf16[512,768]{1,0:T(8,128)(2,1)}, bf16[512,768]{1,0:T(8,128)(2,1)}, u32[]{:S(2)}, u32[]{:S(2)}) collective-permute-start(bf16[512,768]{1,0:T(8,128)(2,1)} %multiply_convert_fusion.1), channel_id=1, source_target_pairs={{0,2},{1,3},{2,0},{3,1},{4,6},{5,7},{6,4},{7,5},{8,10},{9,11},{10,... | collective-permute-start | bytes 2359304 | tf_op jit(solution)/shard_map/ppermute | solution.py:260
  123.4 32.1 %collective-permute-start.15 = (bf16[512,768]{1,0:T(8,128)(2,1)}, bf16[512,768]{1,0:T(8,128)(2,1)}, u32[]{:S(2)}, u32[]{:S(2)}) collective-permute-start(bf16[512,768]{1,0:T(8,128)(2,1)} %param.30), channel_id=1, source_target_pairs={{0,1},{1,0},{2,3},{3,2},{4,5},{5,4},{6,7},{7,6},{8,9},{9,8},{10,11... | collective-permute-start | bytes 2359304 | tf_op jit(solution)/shard_map/ppermute | solution.py:264
  137.0 28.7 %collective-permute-start.16 = (bf16[512,768]{1,0:T(8,128)(2,1)}, bf16[512,768]{1,0:T(8,128)(2,1)}, u32[]{:S(2)}, u32[]{:S(2)}) collective-permute-start(bf16[512,768]{1,0:T(8,128)(2,1)} %collective-permute-done.14), channel_id=1, source_target_pairs={{0,1},{1,0},{2,3},{3,2},{4,5},{5,4},{6,7},{7,6},{8,9},{9,8},{10,11... | collective-permute-start | bytes 2359304 | tf_op jit(solution)/shard_map/ppermute | solution.py:264
  139.1 28.7 %collective-permute-start.10 = (bf16[512,768]{1,0:T(8,128)(2,1)}, bf16[512,768]{1,0:T(8,128)(2,1)}, u32[]{:S(2)}, u32[]{:S(2)}) collective-permute-start(bf16[512,768]{1,0:T(8,128)(2,1)} %multiply_convert_fusion.1), channel_id=1, source_target_pairs={{0,1},{1,0},{2,3},{3,2},{4,5},{5,4},{6,7},{7,6},{8,9},{9,8},{10,11... | collective-permute-start | bytes 2359304 | tf_op jit(solution)/shard_map/ppermute | solution.py:264
  153.4 14.4 %collective-permute-start.11 = (bf16[512,768]{1,0:T(8,128)(2,1)}, bf16[512,768]{1,0:T(8,128)(2,1)}, u32[]{:S(2)}, u32[]{:S(2)}) collective-permute-start(bf16[512,768]{1,0:T(8,128)(2,1)} %collective-permute-done.9), channel_id=1, source_target_pairs={{0,1},{1,0},{2,3},{3,2},{4,5},{5,4},{6,7},{7,6},{8,9},{9,8},{10,11... | collective-permute-start | bytes 2359304 | tf_op jit(solution)/shard_map/ppermute | solution.py:264
  176.8 12.7 %copy-start.16 = (f32[2048,768]{1,0:T(8,128)}, f32[2048,768]{1,0:T(8,128)S(1)}, u32[]{:S(2)}) copy-start(f32[2048,768]{1,0:T(8,128)S(1)} %fusion.28) | copy-start | bytes 18874372
  177.0 21.3 %collective-permute-start.12 = (bf16[2,512,768]{2,1,0:T(8,128)(2,1)S(1)}, bf16[2,512,768]{2,1,0:T(8,128)(2,1)S(1)}, u32[]{:S(2)}, u32[]{:S(2)}) collective-permute-start(bf16[2,512,768]{2,1,0:T(8,128)(2,1)S(1)} %bitcast.123), channel_id=1, source_target_pairs={{0,1},{1,0},{2,3},{3,2},{4,5},{5,4},{6,7},{7,6},{8,9},{9,8},{10,11... | collective-permute-start | bytes 4718600 | tf_op jit(solution)/shard_map/ppermute | solution.py:264
  192.0 9.1 %collective-permute-start.17 = (bf16[2,512,768]{2,1,0:T(8,128)(2,1)S(1)}, bf16[2,512,768]{2,1,0:T(8,128)(2,1)S(1)}, u32[]{:S(2)}, u32[]{:S(2)}) collective-permute-start(bf16[2,512,768]{2,1,0:T(8,128)(2,1)S(1)} %bitcast.122), channel_id=1, source_target_pairs={{0,1},{1,0},{2,3},{3,2},{4,5},{5,4},{6,7},{7,6},{8,9},{9,8},{10,11... | collective-permute-start | bytes 4718600 | tf_op jit(solution)/shard_map/ppermute | solution.py:264
  199.7 20.7 %collective-permute-start.13 = (bf16[512,768]{1,0:T(8,128)(2,1)}, bf16[512,768]{1,0:T(8,128)(2,1)}, u32[]{:S(2)}, u32[]{:S(2)}) collective-permute-start(bf16[512,768]{1,0:T(8,128)(2,1)} %fusion.37), channel_id=1, source_target_pairs={{0,2},{1,3},{2,0},{3,1},{4,6},{5,7},{6,4},{7,5},{8,10},{9,11},{10,... | collective-permute-start | bytes 2359304 | tf_op jit(solution)/shard_map/ppermute | solution.py:260
  204.4 31.8 %collective-permute-start.18 = (bf16[512,768]{1,0:T(8,128)(2,1)}, bf16[512,768]{1,0:T(8,128)(2,1)S(1)}, u32[]{:S(2)}, u32[]{:S(2)}) collective-permute-start(bf16[512,768]{1,0:T(8,128)(2,1)} %fusion.38), channel_id=1, source_target_pairs={{0,2},{1,3},{2,0},{3,1},{4,6},{5,7},{6,4},{7,5},{8,10},{9,11},{10,... | collective-permute-start | bytes 2359304 | tf_op jit(solution)/shard_map/ppermute | solution.py:260
  249.4 13.2 %collective-permute-start.19 = (bf16[2,512,192]{2,1,0:T(8,128)(2,1)}, bf16[2,512,192]{2,1,0:T(8,128)(2,1)S(1)}, u32[]{:S(2)}, u32[]{:S(2)}) collective-permute-start(bf16[2,512,192]{2,1,0:T(8,128)(2,1)} %gather_fusion.2), channel_id=1, source_target_pairs={{0,2},{1,3},{2,0},{3,1},{4,6},{5,7},{6,4},{7,5},{8,10},{9,11},{10,... | collective-permute-start | bytes 1179656 | tf_op jit(solution)/shard_map/ppermute | solution.py:260
  253.4 9.4 %collective-permute-start.25 = (bf16[2,768,192]{1,2,0:T(8,128)(2,1)S(1)}, bf16[2,768,192]{1,2,0:T(8,128)(2,1)S(1)}, u32[]{:S(2)}, u32[]{:S(2)}) collective-permute-start(bf16[2,768,192]{1,2,0:T(8,128)(2,1)S(1)} %slice.331), channel_id=1, source_target_pairs={{0,1},{1,0},{2,3},{3,2},{4,5},{5,4},{6,7},{7,6},{8,9},{9,8},{10,11... | collective-permute-start | bytes 1769480 | tf_op jit(solution)/shard_map/ppermute | solution.py:264
  262.7 2.0 collective-permute-start.20
  263.0 47.6 %collective-permute-start.26 = (bf16[768,192]{0,1:T(8,128)(2,1)S(1)}, bf16[768,192]{0,1:T(8,128)(2,1)S(1)}, u32[]{:S(2)}, u32[]{:S(2)}) collective-permute-start(bf16[768,192]{0,1:T(8,128)(2,1)S(1)} %fusion.50), channel_id=1, source_target_pairs={{0,2},{1,3},{2,0},{3,1},{4,6},{5,7},{6,4},{7,5},{8,10},{9,11},{10,... | collective-permute-start | bytes 884744 | tf_op jit(solution)/shard_map/ppermute | solution.py:260
  265.9 32.3 %copy-start.30 = (bf16[8,96,576]{2,1,0:T(8,128)(2,1)S(1)}, bf16[8,96,576]{2,1,0:T(8,128)(2,1)}, u32[]{:S(2)}) copy-start(bf16[8,96,576]{2,1,0:T(8,128)(2,1)} %copy-done.29) | copy-start | bytes 2654212
  304.1 31.9 %collective-permute-start.21 = (bf16[2,512,768]{2,1,0:T(8,128)(2,1)}, bf16[2,512,768]{2,1,0:T(8,128)(2,1)}, u32[]{:S(2)}, u32[]{:S(2)}) collective-permute-start(bf16[2,512,768]{2,1,0:T(8,128)(2,1)} %bitcast.24), channel_id=1, source_target_pairs={{0,1},{1,0},{2,3},{3,2},{4,5},{5,4},{6,7},{7,6},{8,9},{9,8},{10,11... | collective-permute-start | bytes 4718600 | tf_op jit(solution)/shard_map/ppermute | solution.py:264
  313.3 33.6 %all-to-all-start.1 = ((bf16[8,96,768]{2,1,0:T(8,128)(2,1)}), bf16[8,96,768]{2,1,0:T(8,128)(2,1)}, u32[]{:S(2)}, u32[]{:S(2)}) async-start(bf16[8,96,768]{2,1,0:T(8,128)(2,1)} %pad_maximum_fusion.4), calls=%async_computation.1 | async-start | bytes 2359296 | tf_op jit(solution)/shard_map/all_to_all | solution.py:406
  319.1 16.1 %collective-permute-start.23 = (bf16[2,512,192]{2,1,0:T(8,128)(2,1)}, bf16[2,512,192]{2,1,0:T(8,128)(2,1)S(1)}, u32[]{:S(2)}, u32[]{:S(2)}) collective-permute-start(bf16[2,512,192]{2,1,0:T(8,128)(2,1)} %gather_fusion.3), channel_id=1, source_target_pairs={{2,0},{3,1},{6,4},{7,5},{10,8},{11,9},{14,12},{15,13},{18,16},{19,... | collective-permute-start | bytes 1179656 | tf_op jit(solution)/shard_map/ppermute | solution.py:391
  335.9 16.4 %collective-permute-start.24 = (bf16[512,192]{1,0:T(8,128)(2,1)}, bf16[512,192]{1,0:T(8,128)(2,1)S(1)}, u32[]{:S(2)}, u32[]{:S(2)}) collective-permute-start(bf16[512,192]{1,0:T(8,128)(2,1)} %get-tuple-element.102), channel_id=1, source_target_pairs={{0,1},{1,0},{2,3},{3,2},{4,5},{5,4},{6,7},{7,6},{8,9},{9,8},{10,11... | collective-permute-start | bytes 589832 | tf_op jit(solution)/shard_map/ppermute | solution.py:264
  341.2 26.0 %collective-permute-start.22 = (bf16[512,768]{1,0:T(8,128)(2,1)}, bf16[512,768]{1,0:T(8,128)(2,1)}, u32[]{:S(2)}, u32[]{:S(2)}) collective-permute-start(bf16[512,768]{1,0:T(8,128)(2,1)} %fusion.39), channel_id=1, source_target_pairs={{0,2},{1,3},{2,0},{3,1},{4,6},{5,7},{6,4},{7,5},{8,10},{9,11},{10,... | collective-permute-start | bytes 2359304 | tf_op jit(solution)/shard_map/ppermute | solution.py:260
  349.0 12.4 %collective-permute-start.27 = (f32[96,192]{1,0:T(8,128)}, f32[96,192]{1,0:T(8,128)S(1)}, u32[]{:S(2)}, u32[]{:S(2)}) collective-permute-start(f32[96,192]{1,0:T(8,128)} %slice.243), channel_id=1, source_target_pairs={{0,2},{1,3},{4,6},{5,7},{8,10},{9,11},{12,14},{13,15},{16,18},{17,... | collective-permute-start | bytes 221192 | tf_op jit(solution)/shard_map/ppermute | solution.py:409
  354.7 12.6 %copy-start.41 = (f32[512]{0:T(512)S(1)}, f32[512]{0:T(512)}, u32[]{:S(2)}) copy-start(f32[512]{0:T(512)} %copy-done.40) | copy-start | bytes 6148
  362.1 4.3 %collective-permute-start.28 = (f32[96,192]{1,0:T(8,128)S(1)}, f32[96,192]{1,0:T(8,128)S(1)}, u32[]{:S(2)}, u32[]{:S(2)}) collective-permute-start(f32[96,192]{1,0:T(8,128)S(1)} %get-tuple-element.110), channel_id=1, source_target_pairs={{0,1},{1,0},{2,3},{3,2},{4,5},{5,4},{6,7},{7,6},{8,9},{9,8},{10,11... | collective-permute-start | bytes 221192 | tf_op jit(solution)/shard_map/ppermute | solution.py:264
  373.2 16.0 %all-to-all-start.2 = ((f32[32,1,1540]{2,1,0:T(1,128)}), f32[32,1,1540]{2,1,0:T(1,128)S(1)}, u32[]{:S(2)}, u32[]{:S(2)}) async-start(f32[32,1,1540]{2,1,0:T(1,128)} %broadcast_in_dim.24), calls=%async_computation.2 | async-start | bytes 425984 | tf_op jit(solution)/shard_map/all_to_all | solution.py:419
  379.8 11.9 %copy-start.1 = (bf16[96,384]{1,0:T(8,128)(2,1)S(1)}, bf16[96,384]{1,0:T(8,128)(2,1)}, u32[]{:S(2)}) copy-start(bf16[96,384]{1,0:T(8,128)(2,1)} %param.24) | copy-start | bytes 221188
  (34 other events, 149.6 us)
Sparse Core Ops, SparseCore 0:
  10.3 73.2 all-gather.1
  216.4 67.4 reduce-scatter.3
where the time goes:
time: 405 us; the launch traced here: 399 us
  waiting for transfers between devices  125 us (31%)
  local copies, waits for them, and re-layouts  70.7 us (17%)
  Pallas kernels  55 us (14%)
  matrix products  49.8 us (12%)
  other arithmetic  42.2 us (10%)
  starting transfers between devices  40.1 us (10%)
  between operations  16.7 us (4%)
    ppermute x10, waiting for transfers between devices, swap_x(): return lax.ppermute(v, 'tensor', X_SWAP)  82.1 us
    pallas_call x1, Pallas kernels, attend_back(): pl.pallas_call(backward_kernel, name='attend_back', out_shape=(jax.ShapeD...  32.3 us
    unnamed x101, local copies, waits for them, and re-layouts  30.7 us
    pallas_call x1, Pallas kernels, attend(): pl.pallas_call(forward_kernel, name='attend', out_shape=(jax.ShapeDtypeSt...  22.7 us
    dot_general x4, matrix products, matmul(): return jnp.dot(first_op, second_op, preferred_element_type=jnp.float32)  20.2 us
    dot_general x4, matrix products, matmul_tn(): lax.dot_general(first_op, second_op, (((0,), (0,)), ((), ())), preferred_...  16.3 us
    ppermute x10, starting transfers between devices, swap_x(): return lax.ppermute(v, 'tensor', X_SWAP)  13.9 us
    dot_general x4, matrix products, matmul_nt(): lax.dot_general(first_op, second_op, (((1,), (1,)), ((), ())), preferred_...  13.3 us
  transfers between devices with their start and end apart: 34, of which 17 were waited for; matrix products, arithmetic and copies ran while one was open for 32% of the time, Pallas kernels for 14%

commit v1 on v0

v1 whole, which is shorter than its diff:
```python
import functools
import math

import jax
import jax.numpy as jnp
from jax import lax
from jax.experimental import pallas as pl
from jax.experimental.pallas import tpu as pltpu
from jax.sharding import PartitionSpec as P

HD = 64
EPS = 1e-05
NEG = -1e30
BLK = 256

SMEM = pl.BlockSpec(memory_space=pltpu.SMEM)
VMEM = pl.BlockSpec(memory_space=pltpu.VMEM)


def nt(a, b):
    return lax.dot_general(a, b, (((1,), (1,)), ((), ())), preferred_element_type=jnp.float32)


def nn(a, b):
    return jnp.dot(a, b, preferred_element_type=jnp.float32)


def tn(a, b):
    return lax.dot_general(a, b, (((0,), (0,)), ((), ())), preferred_element_type=jnp.float32)


def call(kernel, name, outs, specs, scratch, flops, exps, args, vmem=56):
    moved = sum(math.prod(v.shape) * v.dtype.itemsize for v in list(args) + list(outs))
    return pl.pallas_call(
        kernel,
        name=name,
        out_shape=tuple(outs),
        in_specs=specs,
        out_specs=tuple(VMEM for _ in outs),
        scratch_shapes=scratch,
        compiler_params=pltpu.CompilerParams(vmem_limit_bytes=vmem << 20),
        cost_estimate=pl.CostEstimate(
            flops=int(flops), transcendentals=int(exps), bytes_accessed=int(moved)
        ),
    )(*args)


def low_shape(*shape):
    return jax.ShapeDtypeStruct(shape, jnp.bfloat16)


def wide_shape(*shape):
    return jax.ShapeDtypeStruct(shape, jnp.float32)


def diag_allowed(picture):
    key_pos = lax.broadcasted_iota(jnp.int32, (BLK, BLK), 0)
    query_pos = lax.broadcasted_iota(jnp.int32, (BLK, BLK), 1)
    return (key_pos <= query_pos) | (picture > 0)


def pick(info_ref, qkv_ref, firsts, rel, kind, head):
    cols = qkv_ref.shape[2] // 3
    lane = kind * cols + head * HD
    part = qkv_ref[rel, :, lane : lane + HD]
    if kind == 2:
        rank = info_ref[0]
        lane = head * HD
        lower = firsts[rel][:, lane : lane + HD]
        upper = firsts[rel][:, cols + lane : cols + lane + HD]
        part = jnp.where(rank < 2, part, jnp.where(rank % 2 == 0, lower, upper))
    return part


def place(info_ref, rel, rows):
    return pl.multiple_of((info_ref[0] ^ rel) * rows, rows)


def prepare(info_ref, qkv_ref, firsts, q_aug, k_aug, head):
    blocks, rows = qkv_ref.shape[:2]
    seq = blocks * rows
    for rel in range(blocks):
        span = pl.ds(place(info_ref, rel, rows), rows)
        part = pick(info_ref, qkv_ref, firsts, rel, 0, head)
        q_aug[head, span, :HD] = part * jnp.bfloat16(1.0 / math.sqrt(HD))
        k_aug[head, span, :HD] = pick(info_ref, qkv_ref, firsts, rel, 1, head)
    pos = lax.broadcasted_iota(jnp.int32, (seq, HD), 0)
    lane = lax.broadcasted_iota(jnp.int32, (seq, HD), 1)
    bias = jnp.where((lane == 0) & (pos >= info_ref[1]), NEG, 0.0)
    k_aug[head, :, HD:] = bias.astype(k_aug.dtype)
    q_aug[head, :, HD:] = jnp.where(lane == 0, 1.0, 0.0).astype(q_aug.dtype)


def forward_kernel(
    info_ref, x0, x1, x2, x3, w_ref, f0, f1, f2, f3,
    qkv_ref, own_ref, core_ref, pair_ref, lse_ref, q_aug, k_aug, v_t, o_t,
):
    inputs, firsts = (x0, x1, x2, x3), (f0, f1, f2, f3)
    blocks, rows = qkv_ref.shape[:2]
    cols = qkv_ref.shape[2] // 3
    heads = cols // HD
    seq = blocks * rows
    for rel in range(blocks):
        qkv_ref[rel] = nn(inputs[rel][...], w_ref[...]).astype(qkv_ref.dtype)
    for head in range(heads):
        prepare(info_ref, qkv_ref, firsts, q_aug, k_aug, head)
        for rel in range(blocks):
            part = pick(info_ref, qkv_ref, firsts, rel, 2, head)
            v_t[head, :, pl.ds(place(info_ref, rel, rows), rows)] = part.T

    def per_head(head, carry):
        for block in range(seq // BLK):
            lo, hi = block * BLK, (block + 1) * BLK
            scores = nt(k_aug[head, :hi, :], q_aug[head, lo:hi, :])
            last = jnp.where(diag_allowed(info_ref[2 + block]), scores[lo:], NEG)
            row_max = jnp.max(last, axis=0, keepdims=True)
            if block:
                row_max = jnp.maximum(row_max, jnp.max(scores[:lo], axis=0, keepdims=True))
            tail = jnp.exp(last - row_max)
            total = jnp.sum(tail, axis=0, keepdims=True)
            acc = nn(v_t[head, :, lo:hi], tail.astype(jnp.bfloat16))
            if block:
                front = jnp.exp(scores[:lo] - row_max)
                total = total + jnp.sum(front, axis=0, keepdims=True)
                acc = acc + nn(v_t[head, :, :lo], front.astype(jnp.bfloat16))
            o_t[head, :, lo:hi] = acc / total
            lse_ref[head, :, lo:hi] = row_max + jnp.log(total)
        return carry

    lax.fori_loop(0, heads, per_head, 0)
    for rel, out in enumerate((own_ref, core_ref, pair_ref.at[0], pair_ref.at[1])):
        part = o_t[:, :, pl.ds(place(info_ref, rel, rows), rows)].reshape(cols, rows)
        out[...] = part.T.astype(out.dtype)


def attend(info, inputs, weights, firsts):
    rows, dim = inputs[0].shape
    cols = weights.shape[1] // 3
    heads = cols // HD
    seq = 4 * rows
    work = heads * seq * (seq + BLK) // 2
    return call(
        forward_kernel,
        "attend",
        [
            low_shape(4, rows, 3 * cols),
            low_shape(rows, cols),
            low_shape(rows, cols),
            low_shape(2, rows, cols),
            wide_shape(heads, 1, seq),
        ],
        [SMEM] + [VMEM] * 9,
        [
            pltpu.VMEM((heads, seq, 2 * HD), jnp.bfloat16),
            pltpu.VMEM((heads, seq, 2 * HD), jnp.bfloat16),
            pltpu.VMEM((heads, HD, seq), jnp.bfloat16),
            pltpu.VMEM((heads, HD, seq), jnp.float32),
        ],
        16 * work * HD + 6 * seq * dim * cols,
        work,
        (info, *inputs, weights, *firsts),
        48,
    )


def backward_kernel(
    info_ref, qkv_ref, f0, f1, f2, f3, g0, g1, g2, g3, own_ref, core_ref, pair_ref, lse_ref,
    dqkv_ref, dv_own, dv_core, dv_pair,
    q_aug, k_aug, v_rows, g_rows, k_t, dq_t, dk_acc, dv_acc, delta,
):
    firsts, grads = (f0, f1, f2, f3), (g0, g1, g2.at[0], g3.at[1])
    outs = (own_ref, core_ref, pair_ref.at[0], pair_ref.at[1])
    dv_outs = (dv_own, dv_core, dv_pair.at[0], dv_pair.at[1])
    blocks, rows = qkv_ref.shape[:2]
    cols = qkv_ref.shape[2] // 3
    heads = cols // HD
    seq = blocks * rows
    for head in range(heads):
        lane = head * HD
        prepare(info_ref, qkv_ref, firsts, q_aug, k_aug, head)
        for rel in range(blocks):
            span = pl.ds(place(info_ref, rel, rows), rows)
            v_rows[head, span, :] = pick(info_ref, qkv_ref, firsts, rel, 2, head)
            k_t[head, :, span] = pick(info_ref, qkv_ref, firsts, rel, 1, head).T
            grad = grads[rel][:, lane : lane + HD]
            g_rows[head, span, :] = grad
            products = grad.astype(jnp.float32) * outs[rel][:, lane : lane + HD].astype(jnp.float32)
            delta[head, :, span] = jnp.sum(products.T, axis=0, keepdims=True)

    def per_head(head, carry):
        dk_acc[head] = jnp.zeros_like(dk_acc[head])
        dv_acc[head] = jnp.zeros_like(dv_acc[head])
        for block in range(seq // BLK):
            lo, hi = block * BLK, (block + 1) * BLK
            q_block = q_aug[head, lo:hi, :]
            g_block = g_rows[head, lo:hi, :]
            lse = lse_ref[head, :, lo:hi]
            shift = delta[head, :, lo:hi]

            def part(start, stop, diagonal):
                probs = jnp.exp(nt(k_aug[head, start:stop, :], q_block) - lse)
                if diagonal:
                    probs = jnp.where(diag_allowed(info_ref[2 + block]), probs, 0.0)
                grad_probs = nt(v_rows[head, start:stop, :], g_block)
                grad_scores = (probs * (grad_probs - shift)).astype(jnp.bfloat16)
                dv_acc[head, start:stop, :] += nn(probs.astype(jnp.bfloat16), g_block)
                dk_acc[head, start:stop, :] += nn(grad_scores, q_block)[:, :HD]
                return nn(k_t[head, :, start:stop], grad_scores)

            acc = part(lo, hi, True)
            if block:
                acc = acc + part(0, lo, False)
            dq_t[head, :, lo:hi] = acc
        return carry

    lax.fori_loop(0, heads, per_head, 0)
    fresh = info_ref[0] < 2
    for rel in range(blocks):
        span = pl.ds(place(info_ref, rel, rows), rows)
        part = dq_t[:, :, span].reshape(cols, rows)
        dqkv_ref[rel, :, :cols] = (part.T * (1.0 / math.sqrt(HD))).astype(dqkv_ref.dtype)
        for head in range(heads):
            lane = head * HD
            dqkv_ref[rel, :, cols + lane : cols + lane + HD] = dk_acc[head, span, :].astype(
                dqkv_ref.dtype
            )
            value = dv_acc[head, span, :].astype(dqkv_ref.dtype)
            dv_outs[rel][:, lane : lane + HD] = value
            kept = jnp.where(fresh, value, jnp.zeros_like(value))
            dqkv_ref[rel, :, 2 * cols + lane : 2 * cols + lane + HD] = kept


def attend_back(info, qkv, firsts, grads, outs, lse):
    rows = qkv.shape[1]
    cols = qkv.shape[2] // 3
    heads = cols // HD
    seq = 4 * rows
    work = heads * seq * (seq + BLK) // 2
    return call(
        backward_kernel,
        "attend_back",
        [
            low_shape(4, rows, 3 * cols),
            low_shape(rows, cols),
            low_shape(rows, cols),
            low_shape(2, rows, cols),
        ],
        [SMEM] + [VMEM] * 13,
        [
            pltpu.VMEM((heads, seq, 2 * HD), jnp.bfloat16),
            pltpu.VMEM((heads, seq, 2 * HD), jnp.bfloat16),
            pltpu.VMEM((heads, seq, HD), jnp.bfloat16),
            pltpu.VMEM((heads, seq, HD), jnp.bfloat16),
            pltpu.VMEM((heads, HD, seq), jnp.bfloat16),
            pltpu.VMEM((heads, HD, seq), jnp.float32),
            pltpu.VMEM((heads, seq, HD), jnp.float32),
            pltpu.VMEM((heads, seq, HD), jnp.float32),
            pltpu.VMEM((heads, 1, seq), jnp.float32),
        ],
        40 * work * HD,
        work,
        (info, qkv, *firsts, *grads, *outs, lse),
    )


def norm_stats(wide):
    centred = wide - jnp.mean(wide, axis=-1, keepdims=True)
    inv_std = lax.rsqrt(jnp.mean(centred * centred, axis=-1, keepdims=True) + EPS)
    return centred * inv_std, inv_std


def valid_rows(info_ref, rows, start, count):
    pos = info_ref[0] * rows + start + lax.broadcasted_iota(jnp.int32, (count, 1), 0)
    return (pos < info_ref[1]).astype(jnp.float32)


def row_sum(v):
    return jnp.sum(v, axis=0, keepdims=True)


def middle_kernel(
    info_ref, tok_ref, h0, h1, h2, h3, w0, w1, w2, w3, gain_ref, resid_ref, input_ref, square_ref
):
    rows = tok_ref.shape[0]
    square = 0.0
    for start in range(0, rows, BLK):
        span = slice(start, start + BLK)
        attn = nt(h0[span], w0[...]) + nt(h1[span], w1[...])
        attn = attn + nt(h2[0, span], w2[...]) + nt(h3[1, span], w3[...])
        resid = tok_ref[span].astype(jnp.float32) + attn
        resid_ref[span] = resid
        normed, _ = norm_stats(resid)
        input_ref[span] = (normed * gain_ref[...]).astype(input_ref.dtype)
        square = square + row_sum(attn * attn * valid_rows(info_ref, rows, start, BLK))
    square_ref[...] = square


def middle(info, tokens, heads, weights, gain):
    rows, dim = tokens.shape
    return call(
        middle_kernel,
        "middle",
        [wide_shape(rows, dim), low_shape(rows, dim), wide_shape(1, dim)],
        [SMEM] + [VMEM] * 10,
        [],
        2 * rows * dim * dim,
        rows,
        (info, tokens, *heads, *weights, gain),
    )


GELU_C = math.sqrt(2.0 / math.pi)
CUBE = 0.044715


def mlp_kernel(with_out, up_cols, x0, x1, c0, c1, w_ref, *refs):
    hid_ref, dup_ref, back_ref = refs[:3]
    rows = x0.shape[0]
    up_w, down_t = w_ref.at[:, :up_cols], w_ref.at[:, up_cols : 2 * up_cols]
    for block, (x_ref, c_ref) in enumerate(((x0, c0), (x1, c1))):
        for start in range(0, rows, BLK):
            span = slice(start, start + BLK)
            up = nn(x_ref[span], up_w[...])
            up2 = up * up
            th = jnp.tanh(GELU_C * up * (1.0 + CUBE * up2))
            half = 0.5 * (1.0 + th)
            hidden = (up * half).astype(jnp.bfloat16)
            hid_ref[block, span] = hidden
            slope = half + 0.5 * up * (1.0 - th * th) * (GELU_C * (1.0 + 3.0 * CUBE * up2))
            dup = (nn(c_ref[span], down_t[...]) * slope).astype(jnp.bfloat16)
            dup_ref[block, span] = dup
            back_ref[block][span] = nt(dup, up_w[...]).astype(jnp.bfloat16)
            if with_out:
                refs[3][block][span] = nt(hidden, down_t[...]).astype(jnp.bfloat16)


def mlp_kernel_full(up_cols, x0, x1, c0, c1, w_ref, hid_ref, dup_ref, b0, b1, o0, o1):
    mlp_kernel(True, up_cols, x0, x1, c0, c1, w_ref, hid_ref, dup_ref, (b0, b1), (o0, o1))


def mlp_kernel_part(up_cols, x0, x1, c0, c1, w_ref, hid_ref, dup_ref, b0, b1):
    mlp_kernel(False, up_cols, x0, x1, c0, c1, w_ref, hid_ref, dup_ref, (b0, b1))


def mlp(xs, cots, weights, up_cols, with_out):
    rows, dim = xs[0].shape
    body = mlp_kernel_full if with_out else mlp_kernel_part
    outs = [low_shape(2, rows, up_cols)] * 2 + [low_shape(rows, dim)] * (4 if with_out else 2)
    return call(
        functools.partial(body, up_cols),
        "mlp_full" if with_out else "mlp_part",
        outs,
        [VMEM] * 5,
        [],
        (8 if with_out else 6) * 2 * rows * dim * up_cols,
        2 * rows * up_cols,
        (*xs, *cots, weights),
    )


def mlp_grads_kernel(up_cols, x0, x1, x2, x3, c0, c1, c2, c3, h_a, h_b, d_a, d_b, w_ref, g_ref, o0, o1):
    down_t = w_ref.at[:, up_cols : 2 * up_cols]
    step = 2 * BLK
    for rel, out in ((0, o0), (1, o1)):
        out[...] = nt(h_b[rel], down_t[...]).astype(out.dtype)
    for start in range(0, up_cols, BLK):
        span = slice(start, start + BLK)
        acc = tn(x0[...], d_a[0, :, span]) + tn(x1[...], d_a[1, :, span])
        acc = acc + tn(x2[...], d_b[0, :, span]) + tn(x3[...], d_b[1, :, span])
        g_ref[:, span] = acc.astype(g_ref.dtype)
        acc = tn(c0[...], h_a[0, :, span]) + tn(c1[...], h_a[1, :, span])
        acc = acc + tn(c2[...], h_b[0, :, span]) + tn(c3[...], h_b[1, :, span])
        g_ref[:, up_cols + start : up_cols + start + BLK] = acc.astype(g_ref.dtype)


def mlp_grads(xs, cots, hid_a, hid_b, dup_a, dup_b, weights, up_cols):
    rows, dim = xs[0].shape
    return call(
        functools.partial(mlp_grads_kernel, up_cols),
        "mlp_grads",
        [low_shape(dim, 2 * up_cols), low_shape(rows, dim), low_shape(rows, dim)],
        [VMEM] * 13,
        [],
        20 * rows * dim * up_cols,
        0,
        (*xs, *cots, hid_a, hid_b, dup_a, dup_b, weights),
    )


def turn_kernel(
    resid_ref, cot_ref, b0, b1, b2, gain_ref, w0, w1, w2, w3,
    grad_ref, low_ref, d_own, d_core, d_pair, gain_out,
):
    rows = resid_ref.shape[0]
    gain_sum = 0.0
    for start in range(0, rows, BLK):
        span = slice(start, start + BLK)
        normed, inv_std = norm_stats(resid_ref[span])
        back = b0[span].astype(jnp.float32) + b1[span].astype(jnp.float32)
        back = back + b2[span].astype(jnp.float32)
        gain_sum = gain_sum + row_sum(back * normed)
        scaled = back * gain_ref[...]
        inner = scaled - jnp.mean(scaled, axis=-1, keepdims=True)
        inner = inner - normed * jnp.mean(scaled * normed, axis=-1, keepdims=True)
        grad = cot_ref[span].astype(jnp.float32) + inner * inv_std
        grad_ref[span] = grad
        low = grad.astype(jnp.bfloat16)
        low_ref[span] = low
        d_own[span] = nn(low, w0[...]).astype(jnp.bfloat16)
        d_core[span] = nn(low, w1[...]).astype(jnp.bfloat16)
        d_pair[0, span] = nn(low, w2[...]).astype(jnp.bfloat16)
        d_pair[1, span] = nn(low, w3[...]).astype(jnp.bfloat16)
    gain_out[...] = gain_sum


def turn(resid, cot, backs, gain, weights):
    rows, dim = cot.shape
    cols = weights[0].shape[1]
    return call(
        turn_kernel,
        "turn",
        [
            wide_shape(rows, dim),
            low_shape(rows, dim),
            low_shape(rows, cols),
            low_shape(rows, cols),
            low_shape(2, rows, cols),
            wide_shape(1, dim),
        ],
        [VMEM] * 10,
        [],
        2 * rows * dim * dim,
        rows,
        (resid, cot, *backs, gain, *weights),
    )


def out_grads_kernel(low_ref, h0, h1, h2, h3, o_near, o_far):
    cols = h0.shape[1]
    low = low_ref[...]
    o_near[0] = tn(low, h0[...])
    o_far[0] = tn(low, h1[...]).astype(jnp.bfloat16)
    o_near[1] = tn(low, h2[0])
    o_far[1] = tn(low, h3[1]).astype(jnp.bfloat16)


def out_grads(low, heads):
    rows, dim = low.shape
    cols = heads[0].shape[1]
    return call(
        out_grads_kernel,
        "out_grads",
        [wide_shape(2, dim, cols), low_shape(2, dim, cols)],
        [VMEM] * 5,
        [],
        2 * rows * dim * dim,
        0,
        (low, *heads),
    )


def input_grads_kernel(dqkv_ref, w_ref, o0, o1, o2, o3):
    for rel, out in ((2, o2), (3, o3), (0, o0), (1, o1)):
        out[...] = nt(dqkv_ref[rel], w_ref[...]).astype(out.dtype)


def input_grads(dqkv, weights):
    rows = dqkv.shape[1]
    dim, cols = weights.shape
    return call(
        input_grads_kernel,
        "input_grads",
        [low_shape(rows, dim)] * 4,
        [VMEM] * 2,
        [],
        8 * rows * dim * cols,
        0,
        (dqkv, weights),
    )


def qkv_grads_kernel(x0, x1, x2, x3, dqkv_ref, out_ref):
    acc = tn(x0[...], dqkv_ref[0]) + tn(x1[...], dqkv_ref[1])
    acc = acc + tn(x2[...], dqkv_ref[2]) + tn(x3[...], dqkv_ref[3])
    out_ref[...] = acc.astype(out_ref.dtype)


def qkv_grads(xs, dqkv):
    rows, dim = xs[0].shape
    cols = dqkv.shape[2]
    return call(
        qkv_grads_kernel,
        "qkv_grads",
        [low_shape(dim, cols)],
        [VMEM] * 5,
        [],
        8 * rows * dim * cols,
        0,
        (*xs, dqkv),
    )[0]


def finish_kernel(tok_ref, grad_ref, b0, b1, b2, gain_ref, out_ref, gain_out):
    rows = tok_ref.shape[0]
    gain_sum = 0.0
    for start in range(0, rows, BLK):
        span = slice(start, start + BLK)
        normed, inv_std = norm_stats(tok_ref[span].astype(jnp.float32))
        back = b0[span].astype(jnp.float32) + b1[span].astype(jnp.float32)
        back = back + b2[span].astype(jnp.float32)
        gain_sum = gain_sum + row_sum(back * normed)
        scaled = back * gain_ref[...]
        inner = scaled - jnp.mean(scaled, axis=-1, keepdims=True)
        inner = inner - normed * jnp.mean(scaled * normed, axis=-1, keepdims=True)
        out_ref[span] = grad_ref[span] + inner * inv_std
    gain_out[...] = gain_sum


def finish(tokens, grad, backs, gain):
    rows, dim = tokens.shape
    return call(
        finish_kernel,
        "finish",
        [wide_shape(rows, dim), wide_shape(1, dim)],
        [VMEM] * 6,
        [],
        rows * dim * 20,
        rows,
        (tokens, grad, *backs, gain),
    )


def output_kernel(info_ref, resid_ref, b0, b1, b2, out_ref, final_sq, mlp_sq):
    rows = resid_ref.shape[0]
    sum_final, sum_mlp = 0.0, 0.0
    for start in range(0, rows, BLK):
        span = slice(start, start + BLK)
        valid = valid_rows(info_ref, rows, start, BLK)
        mlp_out = b0[span].astype(jnp.float32) + b1[span].astype(jnp.float32)
        mlp_out = mlp_out + b2[span].astype(jnp.float32)
        final = resid_ref[span] + mlp_out
        out_ref[span] = final.astype(out_ref.dtype)
        sum_final = sum_final + row_sum(final * final * valid)
        sum_mlp = sum_mlp + row_sum(mlp_out * mlp_out * valid)
    final_sq[...] = sum_final
    mlp_sq[...] = sum_mlp


def output(info, resid, parts):
    rows, dim = resid.shape
    return call(
        output_kernel,
        "output",
        [low_shape(rows, dim), wide_shape(1, dim), wide_shape(1, dim)],
        [SMEM] + [VMEM] * 4,
        [],
        rows * dim * 10,
        0,
        (info, resid, *parts),
    )


X_SWAP = [(0, 2), (1, 3), (2, 0), (3, 1)]
CORE_SWAP = [(0, 1), (1, 0), (2, 3), (3, 2)]


def swap_x(v):
    return lax.ppermute(v, "tensor", X_SWAP)


def swap_core(v):
    return lax.ppermute(v, "tensor", CORE_SWAP)


def tied(value, *others):
    return lax.optimization_barrier((value, *others))[0]


def plus(a, b):
    return (a.astype(jnp.float32) + b.astype(jnp.float32)).astype(jnp.bfloat16)


def body(
    tokens,
    first_values,
    pieces,
    lengths,
    w_query,
    w_key,
    w_value,
    w_out,
    w_up,
    w_down,
    gain_attn,
    gain_mlp,
    cotangent,
):
    dp_size = lax.axis_size("dp")
    rank = lax.axis_index("tensor")
    core = rank % 2
    rows, dim = tokens.shape
    shard, cols = w_query.shape
    up_cols = w_up.shape[1]
    info = jnp.concatenate([rank[None].astype(jnp.int32), lengths, pieces[::BLK]])
    gain_one, gain_two = gain_attn[None], gain_mlp[None]

    value_cols = jnp.where(core == 0, w_value[:, :cols], w_value[:, cols:])
    early = jnp.concatenate([w_query, w_key, value_cols], axis=1)
    late = jnp.concatenate([w_up, w_down.T, w_out.T], axis=1)
    late_all = lax.all_gather(late, "dp", axis=0, tiled=True)
    early_all = lax.all_to_all(
        jnp.broadcast_to(early[None], (dp_size,) + early.shape), "dp", 0, 0
    ).reshape(dim, 3 * cols)
    tok_x = swap_x(tokens)
    tok_core = swap_core(tokens)
    tok_diag = swap_core(tok_x)
    first_x = lax.ppermute(first_values, "tensor", [(0, 2), (1, 3)])
    firsts = (first_values, swap_core(first_values), first_x, swap_core(first_x))

    def normed_low(v):
        normed, _ = norm_stats(v.astype(jnp.float32))
        return (normed * gain_one).astype(jnp.bfloat16)

    xs = tuple(normed_low(v) for v in (tokens, tok_core, tok_x, tok_diag))
    qkv, h_own, h_core, h_pair, lse = attend(info, xs, early_all, firsts)

    cot_x = swap_x(tied(cotangent, tok_x, first_x))
    out_own = late_all[:, 2 * up_cols :]
    out_x = swap_x(out_own)
    h_pair, h_core = lax.optimization_barrier((h_pair, h_core, cot_x))[:2]
    cot_core = swap_core(cotangent)
    cot_diag = swap_core(cot_x)
    outs = (out_own, swap_core(out_own), out_x, swap_core(out_x))

    from_x = swap_x(h_pair)
    heads_mine = (h_own, swap_core(h_core), from_x, swap_core(from_x))
    resid, mlp_in, attn_sq = middle(info, tokens, heads_mine, outs, gain_two)
    in_x = swap_x(mlp_in)
    in_core = swap_core(mlp_in)
    hid_a, dup_a, back_own, back_core, out_0, out_1 = mlp(
        (mlp_in, in_core), (cotangent, cot_core), late_all, up_cols, True
    )
    in_diag = swap_core(in_x)
    back_1 = swap_core(back_core)
    out_near = swap_core(out_1)
    hid_b, dup_b, back_x, back_diag = mlp((in_x, in_diag), (cot_x, cot_diag), late_all, up_cols, False)
    back_2 = swap_x(plus(back_x, swap_core(back_diag)))
    grads_mlp, out_2, out_3 = mlp_grads(
        (mlp_in, in_core, in_x, in_diag),
        (cotangent, cot_core, cot_x, cot_diag),
        hid_a, hid_b, dup_a, dup_b, late_all, up_cols,
    )
    mlp_share = lax.psum_scatter(grads_mlp, "dp", scatter_dimension=0, tiled=True)
    out_sum = plus(out_2, swap_core(out_3))

    resid_grad, resid_low, d_own, d_core, d_pair, gain_two_sum = turn(
        resid, cotangent, (back_own, back_1, back_2), gain_two, outs
    )
    d_x = swap_x(d_pair)
    grads_heads = (d_own, swap_core(d_core), d_x, swap_core(d_x))
    near, far = out_grads(resid_low, heads_mine)
    far = swap_core(far)
    dqkv, dv_own, dv_core, dv_pair = attend_back(
        info, qkv, firsts, grads_heads, (h_own, h_core, h_pair), lse
    )
    out_from_x = swap_x(tied(out_sum, d_x))
    near_x = swap_x(plus(near[1], far[1]))
    dqkv, dv_pair = lax.optimization_barrier((dqkv, dv_pair, out_from_x, near_x))[:2]

    b_0, b_1, b_2, b_3 = input_grads(dqkv, early_all)
    b_from_x = swap_x(plus(b_2, swap_core(b_3)))
    b_from_core = swap_core(b_1)
    grad_out_t = (near[0] + far[0].astype(jnp.float32) + near_x.astype(jnp.float32)).astype(jnp.bfloat16)
    grads_qkv = qkv_grads(xs, dqkv)
    tail = jnp.concatenate([grads_qkv, grad_out_t], axis=1).reshape(dp_size, shard, 4 * cols)
    tail_all = lax.all_to_all(tail, "dp", 0, 0)

    final, final_sq, mlp_sq = output(info, resid, (out_0, out_near, out_from_x))
    first_from_x = lax.ppermute(tied(dv_pair, b_from_x), "tensor", [(2, 0), (3, 1)])
    first_a = jnp.where(rank < 2, first_from_x[0], dv_own)
    first_b = swap_core(jnp.where(rank < 2, first_from_x[1], dv_core))
    first_grad = jnp.where(
        core == 0,
        jnp.concatenate([first_a, first_b], axis=1),
        jnp.concatenate([first_b, first_a], axis=1),
    ).astype(jnp.float32)
    token_grad, gain_one_sum = finish(tokens, resid_grad, (b_0, b_from_core, b_from_x), gain_one)

    tail_share = jnp.sum(tail_all.astype(jnp.float32), axis=0)
    value_own = tail_share[:, 2 * cols : 3 * cols]
    value_x = lax.ppermute(value_own, "tensor", [(0, 2), (1, 3)])
    value_here = jnp.where(rank < 2, value_own, value_x)
    value_peer = swap_core(value_here)
    value_share = jnp.where(
        core == 0,
        jnp.concatenate([value_here, value_peer], axis=1),
        jnp.concatenate([value_peer, value_here], axis=1),
    )
    positions = rank * rows + lax.iota(jnp.int32, rows)
    count = jnp.sum((positions < lengths[0]).astype(jnp.float32))
    squares = jnp.stack([jnp.sum(final_sq), jnp.sum(attn_sq), jnp.sum(mlp_sq), count])
    small = jnp.concatenate([gain_one_sum[0], gain_two_sum[0], squares])
    everyone = dp_size * 4
    small_all = lax.all_to_all(
        jnp.broadcast_to(small[None], (everyone,) + small.shape), ("dp", "tensor"), 0, 0
    )
    total = jnp.sum(small_all, axis=0)
    square_total = total[2 * dim :]
    rms = jnp.sqrt(square_total[:3] / (square_total[3] * dim))
    mlp_wide = mlp_share.astype(jnp.float32)
    return (
        final,
        token_grad,
        first_grad,
        tail_share[:, :cols],
        tail_share[:, cols : 2 * cols],
        value_share,
        tail_share[:, 3 * cols :].T,
        mlp_wide[:, :up_cols],
        mlp_wide[:, up_cols:].T,
        total[:dim],
        total[dim : 2 * dim],
        rms,
    )


def solution(mesh):
    in_specs = (
        P(("dp", "tensor"), None),
        P(("dp", "tensor"), None),
        P("dp"),
        P("dp"),
        P("dp", "tensor"),
        P("dp", "tensor"),
        P("dp", None),
        P("tensor", "dp"),
        P("dp", "tensor"),
        P("tensor", "dp"),
        P(),
        P(),
        P(("dp", "tensor"), None),
    )
    out_specs = (
        P(("dp", "tensor"), None),
        P(("dp", "tensor"), None),
        P(("dp", "tensor"), None),
        P("dp", "tensor"),
        P("dp", "tensor"),
        P("dp", None),
        P("tensor", "dp"),
        P("dp", "tensor"),
        P("tensor", "dp"),
        P(),
        P(),
        P(),
    )
    return jax.shard_map(body, mesh=mesh, in_specs=in_specs, out_specs=out_specs, check_vma=False)
```

time: 405 us -> 361 us (0.89)
  Pallas kernels: 55 us -> 130 us
  matrix products: 49.8 us -> 0 us
  local copies, waits for them, and re-layouts: 70.7 us -> 25.6 us
  other arithmetic: 42.2 us -> 23.4 us
    pallas_call x2 -> x12, Pallas kernels: 55 us -> 130 us  [call(): pl.pallas_call(kernel, name=name, out_shape=tuple(outs), in_specs=specs,...]
    dot_general x12 -> x0, matrix products: 49.8 us -> none  [the longest x4 20.2 us: matmul(): return jnp.dot(first_op, second_op, preferred_element_type=jnp.float32)]
    unnamed x101 -> x92, local copies, waits for them, and re-layouts: 30.7 us -> 11.1 us
    ppermute x10, waiting for transfers between devices: 82.1 us -> 68.3 us  [swap_x(): return lax.ppermute(v, 'tensor', X_SWAP)]
    all_to_all x2, waiting for transfers between devices: 11.5 us -> 22.1 us  [the longest x1 21.6 us: body(): tail_all = lax.all_to_all(tail, 'dp', 0, 0)]
    add x6 -> x0, other arithmetic: 8.94 us -> none  [the longest x4 3.53 us: scatter_rel(): pair = parts[0:2] + from_core]
    all_to_all x1, waiting for transfers between devices: 7.75 us -> 16.6 us  [body(): lax.all_to_all(jnp.broadcast_to(early[None], (dp_size,) + early.shape), '...]
    ppermute x1, waiting for transfers between devices: 8.46 us -> 0.01 us  [body(): lax.ppermute(tied(dv_pair, b_from_x), 'tensor', [(2, 0), (3, 1)])]
  transfers between devices with their start and end apart: 34 -> 41, of which waited for: 17 -> 14; matrix products, arithmetic and copies ran while one was open for 32% -> 11% of each run, Pallas kernels for 14% -> 35%
where the time goes in v1:
time: 361 us; the launch traced here: 356 us
  Pallas kernels  130 us (36%)
  waiting for transfers between devices  123 us (34%)
  starting transfers between devices  37.6 us (10%)
  local copies, waits for them, and re-layouts  25.6 us (7%)
  other arithmetic  23.4 us (6%)
  between operations  16.4 us (5%)
    pallas_call x12, Pallas kernels, call(): pl.pallas_call(kernel, name=name, out_shape=tuple(outs), in_specs=specs,...  130 us
    ppermute x10, waiting for transfers between devices, swap_x(): return lax.ppermute(v, 'tensor', X_SWAP)  68.3 us
    all_to_all x1, waiting for transfers between devices, body(): tail_all = lax.all_to_all(tail, 'dp', 0, 0)  21.6 us
    all_to_all x1, waiting for transfers between devices, body(): lax.all_to_all(jnp.broadcast_to(early[None], (dp_size,) + early.shape), '...  16.6 us
    ppermute x10, starting transfers between devices, swap_x(): return lax.ppermute(v, 'tensor', X_SWAP)  11.2 us
    unnamed x92, local copies, waits for them, and re-layouts  11.1 us
    ppermute x1, waiting for transfers between devices, body(): first_x = lax.ppermute(first_values, 'tensor', [(0, 2), (1, 3)])  8.55 us
  transfers between devices with their start and end apart: 41, of which 14 were waited for; matrix products, arithmetic and copies ran while one was open for 11% of the time, Pallas kernels for 35%

profile of v1, /device:TPU:0, one launch (start us, length us, event | category | flops | bytes accessed | tf_op | source)
XLA Modules:
  0.0 356.4 jit_solution(7334607467887641761)
XLA Ops:
  7.2 3.0 collective-permute-start.1
  10.2 2.8 collective-permute-start.4
  14.1 1.7 pad_maximum_fusion.1
  18.8 6.3 %all-to-all-start = ((bf16[8,96,576]{2,1,0:T(8,128)(2,1)}), bf16[8,96,576]{2,1,0:T(8,128)(2,1)}, u32[]{:S(2)}, u32[]{:S(2)}) async-start(bf16[8,96,576]{2,1,0:T(8,128)(2,1)} %broadcast_in_dim.11), calls=%async_computation | async-start | bytes 1966080 | tf_op jit(solution)/shard_map/all_to_all | solution.py:611
  27.2 8.5 %collective-permute-done.4.f2 = bf16[512,384]{1,0:T(8,128)(2,1)} collective-permute-done((bf16[512,384]{1,0:T(8,128)(2,1)}, bf16[512,384]{1,0:T(8,128)(2,1)}, u32[]{:S(2)}, u32[]{:S(2)}) %collective-permute-start.4) | collective-permute-done | bytes 393248 | tf_op jit(solution)/shard_map/ppermute | solution.py:617
  37.1 2.5 collective-permute-start.6
  41.1 2.4 fusion.10
  44.4 16.6 %all-to-all-done = bf16[8,96,576]{2,1,0:T(8,128)(2,1)} async-done(((bf16[8,96,576]{2,1,0:T(8,128)(2,1)}), bf16[8,96,576]{2,1,0:T(8,128)(2,1)}, u32[]{:S(2)}, u32[]{:S(2)}) %all-to-all-start) | async-done | bytes 884768 | tf_op jit(solution)/shard_map/all_to_all | solution.py:611
  62.0 27.2 %attend.1 = (bf16[4,512,576]{2,1,0:T(8,128)(2,1)}, bf16[512,192]{1,0:T(8,128)(2,1)S(1)}, bf16[512,192]{1,0:T(8,128)(2,1)S(1)}, bf16[2,512,192]{2,1,0:T(8,128)(2,1)}, f32[3,1,2048]{2,1,0:T(1,128)S(1)}) custom-call(s32[10]{0:T(128)S(1)} %pad_add_fusion.info_ref, bf16[512,768]{1,0:T(8,128)(2,1)S(1)} %get-tuple-element.171.x0, ...), custom_call_target="tpu_custom_call" | custom-call | flops 9059696640 | bytes 8773672 | tf_op jit(solution)/shard_map/attend/pallas_call | solution.py:34
  91.2 1.0 slice.83.w0
  92.3 2.1 collective-permute-start.11
  94.4 11.9 %collective-permute-done.8.h2 = bf16[2,512,192]{2,1,0:T(8,128)(2,1)S(1)} collective-permute-done((bf16[2,512,192]{2,1,0:T(8,128)(2,1)}, bf16[2,512,192]{2,1,0:T(8,128)(2,1)S(1)}, u32[]{:S(2)}, u32[]{:S(2)}) %collective-permute-start.8) | collective-permute-done | bytes 393248 | tf_op jit(solution)/shard_map/ppermute | solution.py:568
  106.7 6.9 %collective-permute-done.11.w2 = bf16[768,192]{1,0:T(8,128)(2,1)S(1)} collective-permute-done((bf16[768,192]{1,0:T(8,128)(2,1)S(1)}, bf16[768,192]{1,0:T(8,128)(2,1)S(1)}, u32[]{:S(2)}, u32[]{:S(2)}) %collective-permute-start.11) | collective-permute-done | bytes 294944 | tf_op jit(solution)/shard_map/ppermute | solution.py:568
  114.7 1.1 collective-permute-done.7.h1
  117.0 4.6 %middle.1 = (f32[512,768]{1,0:T(8,128)}, bf16[512,768]{1,0:T(8,128)(2,1)}, f32[1,768]{1,0:T(1,128)}) custom-call(s32[10]{0:T(128)} %copy-done.5, bf16[512,768]{1,0:T(8,128)(2,1)} %tok_ref.3, bf16[512,192]{1,0:T(8,128)(2,1)} %copy-done.4, bf16[512,192]{1,0:T(8,128)(2,1)} %copy-done.23, bf16[2,512,192]{2,1,0:T(8,128)(2,1)} %copy-done.17, ...), custom_call_target="tpu_custom_call" | custom-call | flops 603979776 | bytes 5511208 | tf_op jit(solution)/shard_map/middle/pallas_call | solution.py:34
  121.8 19.5 %collective-permute-done.16.x0.x2 = bf16[512,768]{1,0:T(8,128)(2,1)S(1)} collective-permute-done((bf16[512,768]{1,0:T(8,128)(2,1)}, bf16[512,768]{1,0:T(8,128)(2,1)S(1)}, u32[]{:S(2)}, u32[]{:S(2)}) %collective-permute-start.16) | collective-permute-done | bytes 786464 | tf_op jit(solution)/shard_map/ppermute | solution.py:568
  141.9 2.9 collective-permute-done.17.x1.x3
  145.7 9.0 %mlp_part.1 = (bf16[2,512,768]{2,1,0:T(8,128)(2,1)}, bf16[2,512,768]{2,1,0:T(8,128)(2,1)}, bf16[512,768]{1,0:T(8,128)(2,1)}, bf16[512,768]{1,0:T(8,128)(2,1)}) custom-call(bf16[512,768]{1,0:T(8,128)(2,1)} %copy-done.38, bf16[512,768]{1,0:T(8,128)(2,1)} %copy-done.40, bf16[512,768]{1,0:T(8,128)(2,1)} %collective-permute-done.6.c0.c2, ...), custom_call_target="tpu_custom_call" | custom-call | flops 3623878656 | bytes 10518528 | tf_op jit(solution)/shard_map/mlp_part/pallas_call | solution.py:34
  156.6 10.8 %mlp_full.1 = (bf16[2,512,768]{2,1,0:T(8,128)(2,1)}, bf16[2,512,768]{2,1,0:T(8,128)(2,1)}, bf16[512,768]{1,0:T(8,128)(2,1)}, bf16[512,768]{1,0:T(8,128)(2,1)}, b...) custom-call(bf16[512,768]{1,0:T(8,128)(2,1)} %get-tuple-element.68.x0, bf16[512,768]{1,0:T(8,128)(2,1)} %copy-done.42, ...), custom_call_target="tpu_custom_call" | custom-call | flops 4831838208 | bytes 12091392 | tf_op jit(solution)/shard_map/mlp_full/pallas_call | solution.py:34
  168.5 13.2 %mlp_grads.1 = (bf16[768,1536]{1,0:T(8,128)(2,1)}, bf16[512,768]{1,0:T(8,128)(2,1)}, bf16[512,768]{1,0:T(8,128)(2,1)}) custom-call(bf16[512,768]{1,0:T(8,128)(2,1)} %get-tuple-element.68.x0, bf16[512,768]{1,0:T(8,128)(2,1)} %copy-done.42, bf16[512,768]{1,0:T(8,128)(2,1)} %copy-done.38, bf16[512,768]{1,0:T(8,128)(2,1)} %copy-done.40, ...), custom_call_target="tpu_custom_call" | custom-call | flops 6039797760 | bytes 19169280 | tf_op jit(solution)/shard_map/mlp_grads/pallas_call | solution.py:34
  181.7 6.1 %collective-permute-done.22.b2 = bf16[512,768]{1,0:T(8,128)(2,1)S(1)} collective-permute-done((bf16[512,768]{1,0:T(8,128)(2,1)S(1)}, bf16[512,768]{1,0:T(8,128)(2,1)S(1)}, u32[]{:S(2)}, u32[]{:S(2)}) %collective-permute-start.22) | collective-permute-done | bytes 786464 | tf_op jit(solution)/shard_map/ppermute | solution.py:568
  188.7 6.1 %turn.1 = (f32[512,768]{1,0:T(8,128)}, bf16[512,768]{1,0:T(8,128)(2,1)}, bf16[512,192]{1,0:T(8,128)(2,1)}, bf16[512,192]{1,0:T(8,128)(2,1)}, bf16[2,512,192]{2,1,0:T(8,128)(2,1)}, /*index=5*/f32[1,768]{1,0:T(1,128)}) custom-call(f32[512,768]{1,0:T(8,128)} %get-tuple-element.67.resid_ref, bf16[512,768]{1,0:T(8,128)(2,1)} %cot_ref.1, ...), custom_call_target="tpu_custom_call" | custom-call | flops 603979776 | bytes 9050112 | tf_op jit(solution)/shard_map/turn/pallas_call | solution.py:34
  194.7 4.0 %out_grads.1 = (f32[2,768,192]{2,1,0:T(8,128)}, bf16[2,768,192]{2,1,0:T(8,128)(2,1)}) custom-call(bf16[512,768]{1,0:T(8,128)(2,1)} %get-tuple-element.91.low_ref, bf16[512,192]{1,0:T(8,128)(2,1)} %copy-done.4, bf16[512,192]{1,0:T(8,128)(2,1)} %copy-done.23, bf16[2,512,192]{2,1,0:T(8,128)(2,1)} %copy-done.17, bf16[2,512,192]{2,1,0:T(8,128)(2,1)} %copy-done.18), custom_call_target="tpu_custom_call" | custom-call | flops 603979776 | bytes 3735552 | tf_op jit(solution)/shard_map/out_grads/pallas_call | solution.py:34
  198.7 2.3 copy.40
  201.4 1.1 add_convert_fusion.2
  202.7 13.0 %collective-permute-done.23.g2 = bf16[2,512,192]{2,1,0:T(8,128)(2,1)} collective-permute-done((bf16[2,512,192]{2,1,0:T(8,128)(2,1)}, bf16[2,512,192]{2,1,0:T(8,128)(2,1)}, u32[]{:S(2)}, u32[]{:S(2)}) %collective-permute-start.23) | collective-permute-done | bytes 393248 | tf_op jit(solution)/shard_map/ppermute | solution.py:568
  216.0 1.1 fusion.26
  217.3 1.8 collective-permute-start.28
  219.2 33.8 %attend_back.1 = (bf16[4,512,576]{2,1,0:T(8,128)(2,1)}, bf16[512,192]{1,0:T(8,128)(2,1)}, bf16[512,192]{1,0:T(8,128)(2,1)}, bf16[2,512,192]{2,1,0:T(8,128)(2,1)}) custom-call(s32[10]{0:T(128)} %copy-done.5, bf16[4,512,576]{2,1,0:T(8,128)(2,1)} %get-tuple-element.85.qkv_ref, bf16[512,384]{1,0:T(8,128)(2,1)} %f0.3, ...), custom_call_target="tpu_custom_call" | custom-call | flops 18119393280 | bytes 9068584 | tf_op jit(solution)/shard_map/attend_back/pallas_call | solution.py:34
  253.0 6.3 %input_grads.1 = (bf16[512,768]{1,0:T(8,128)(2,1)}, bf16[512,768]{1,0:T(8,128)(2,1)}, bf16[512,768]{1,0:T(8,128)(2,1)}, bf16[512,768]{1,0:T(8,128)(2,1)}) custom-call(bf16[4,512,576]{2,1,0:T(8,128)(2,1)} %get-tuple-element.94.dqkv_ref, bf16[768,576]{1,0:T(8,128)(2,1)} %bitcast.1.w_ref), custom_call_target="tpu_custom_call" | custom-call | flops 1811939328 | bytes 6389760 | tf_op jit(solution)/shard_map/input_grads/pallas_call | solution.py:34
  260.3 1.7 collective-permute-done.30
  262.0 2.2 add_convert_fusion
  266.8 3.9 %output.1 = (bf16[512,768]{1,0:T(8,128)(2,1)}, f32[1,768]{1,0:T(1,128)}, f32[1,768]{1,0:T(1,128)}) custom-call(s32[10]{0:T(128)} %copy-done.5, f32[512,768]{1,0:T(8,128)} %get-tuple-element.67.resid_ref, bf16[512,768]{1,0:T(8,128)(2,1)} %get-tuple-element.69.b0, bf16[512,768]{1,0:T(8,128)(2,1)} %collective-permute-done.15.b1, bf16[512,768]{1,0:T(8,128)(2,1)} %copy-done.27), custom_call_target="tpu_custom_call" | custom-call | flops 3932160 | bytes 4724776 | tf_op jit(solution)/shard_map/output/pallas_call | solution.py:34
  270.7 1.3 reduce_sum.135
  272.0 1.3 reduce_sum.137
  273.3 10.9 %collective-permute-done.31.b2 = bf16[512,768]{1,0:T(8,128)(2,1)} collective-permute-done((bf16[512,768]{1,0:T(8,128)(2,1)}, bf16[512,768]{1,0:T(8,128)(2,1)}, u32[]{:S(2)}, u32[]{:S(2)}) %collective-permute-start.31) | collective-permute-done | bytes 786464 | tf_op jit(solution)/shard_map/ppermute | solution.py:568
  284.3 4.8 %finish.1 = (f32[512,768]{1,0:T(8,128)}, f32[1,768]{1,0:T(1,128)}) custom-call(bf16[512,768]{1,0:T(8,128)(2,1)} %tok_ref.3, f32[512,768]{1,0:T(8,128)} %get-tuple-element.84.grad_ref, bf16[512,768]{1,0:T(8,128)(2,1)} %get-tuple-element.95.b0, bf16[512,768]{1,0:T(8,128)(2,1)} %copy-done.24, bf16[512,768]{1,0:T(8,128)(2,1)} %collective-permute-done.31.b2, ...), custom_call_target="tpu_custom_call" | custom-call | flops 7864320 | bytes 6297600 | tf_op jit(solution)/shard_map/finish/pallas_call | solution.py:34
  289.8 2.7 concatenate.35
  293.3 2.9 all-to-all-start.2
  296.3 6.3 %qkv_grads.1 = bf16[768,576]{1,0:T(8,128)(2,1)} custom-call(bf16[512,768]{1,0:T(8,128)(2,1)} %copy-done.3, bf16[512,768]{1,0:T(8,128)(2,1)} %copy-done.1, bf16[512,768]{1,0:T(8,128)(2,1)} %copy-done.2, bf16[512,768]{1,0:T(8,128)(2,1)} %copy-done, bf16[4,512,576]{2,1,0:T(8,128)(2,1)} %get-tuple-element.94.dqkv_ref), custom_call_target="tpu_custom_call" | custom-call | flops 1811939328 | bytes 6389760 | tf_op jit(solution)/shard_map/qkv_grads/pallas_call | solution.py:34
  302.6 2.5 pad_maximum_fusion
  305.5 5.5 %all-to-all-start.1 = ((bf16[8,96,768]{2,1,0:T(8,128)(2,1)}), bf16[8,96,768]{2,1,0:T(8,128)(2,1)S(1)}, u32[]{:S(2)}, u32[]{:S(2)}) async-start(bf16[8,96,768]{2,1,0:T(8,128)(2,1)} %bitcast.8), calls=%async_computation.1 | async-start | bytes 2359296 | tf_op jit(solution)/shard_map/all_to_all | solution.py:676
  311.0 1.3 collective-permute-start.32
  315.8 1.7 slice.92
  318.3 21.6 %all-to-all-done.1 = bf16[8,96,768]{2,1,0:T(8,128)(2,1)S(1)} async-done(((bf16[8,96,768]{2,1,0:T(8,128)(2,1)}), bf16[8,96,768]{2,1,0:T(8,128)(2,1)S(1)}, u32[]{:S(2)}, u32[]{:S(2)}) %all-to-all-start.1) | async-done | bytes 1179680 | tf_op jit(solution)/shard_map/all_to_all | solution.py:676
  340.1 3.4 collective-permute-start.34
  343.6 2.0 collective-permute-done.34
  347.1 1.1 fusion.22
  (195 shorter events, 33.2 us)
Async XLA Ops:
  7.2 84.1 %all-gather.2.cloned.1.call-start = ((), (), s32[]{:S(2)}) async-start(), calls=%async_computation.4 | async-start | bytes 3096576 | tf_op jit(solution)/shard_map/all_gather | solution.py:610
  7.2 28.6 %collective-permute-start.1 = (bf16[512,768]{1,0:T(8,128)(2,1)}, bf16[512,768]{1,0:T(8,128)(2,1)S(1)}, u32[]{:S(2)}, u32[]{:S(2)}) collective-permute-start(bf16[512,768]{1,0:T(8,128)(2,1)} %tok_ref.3), channel_id=1, source_target_pairs={{0,2},{1,3},{2,0},{3,1},{4,6},{5,7},{6,4},{7,5},{8,10},{9,11},{10,... | collective-permute-start | bytes 2359304 | tf_op jit(solution)/shard_map/ppermute | solution.py:568
  10.2 26.6 %collective-permute-start = (bf16[512,768]{1,0:T(8,128)(2,1)}, bf16[512,768]{1,0:T(8,128)(2,1)S(1)}, u32[]{:S(2)}, u32[]{:S(2)}) collective-permute-start(bf16[512,768]{1,0:T(8,128)(2,1)} %tok_ref.3), channel_id=1, source_target_pairs={{0,1},{1,0},{2,3},{3,2},{4,5},{5,4},{6,7},{7,6},{8,9},{9,8},{10,11... | collective-permute-start | bytes 2359304 | tf_op jit(solution)/shard_map/ppermute | solution.py:572
  10.2 25.5 %collective-permute-start.4 = (bf16[512,384]{1,0:T(8,128)(2,1)}, bf16[512,384]{1,0:T(8,128)(2,1)}, u32[]{:S(2)}, u32[]{:S(2)}) collective-permute-start(bf16[512,384]{1,0:T(8,128)(2,1)} %f0.3), channel_id=1, source_target_pairs={{0,2},{1,3},{4,6},{5,7},{8,10},{9,11},{12,14},{13,15},{16,18},{17,... | collective-permute-start | bytes 1179656 | tf_op jit(solution)/shard_map/ppermute | solution.py:617
  13.0 30.5 %collective-permute-start.3 = (bf16[512,384]{1,0:T(8,128)(2,1)}, bf16[512,384]{1,0:T(8,128)(2,1)}, u32[]{:S(2)}, u32[]{:S(2)}) collective-permute-start(bf16[512,384]{1,0:T(8,128)(2,1)} %f0.3), channel_id=1, source_target_pairs={{0,1},{1,0},{2,3},{3,2},{4,5},{5,4},{6,7},{7,6},{8,9},{9,8},{10,11... | collective-permute-start | bytes 1179656 | tf_op jit(solution)/shard_map/ppermute | solution.py:572
  18.8 42.1 %all-to-all-start = ((bf16[8,96,576]{2,1,0:T(8,128)(2,1)}), bf16[8,96,576]{2,1,0:T(8,128)(2,1)}, u32[]{:S(2)}, u32[]{:S(2)}) async-start(bf16[8,96,576]{2,1,0:T(8,128)(2,1)} %broadcast_in_dim.11), calls=%async_computation | async-start | bytes 1966080 | tf_op jit(solution)/shard_map/all_to_all | solution.py:611
  25.1 289.7 %reduce-scatter.2.cloned.1.call-start = ((), (), s32[]{:S(2)}) async-start(), calls=%async_computation.5 | async-start | bytes 2654208 | tf_op jit(solution)/shard_map/reduce_scatter | solution.py:653
  27.2 33.7 %copy-start.5 = (s32[10]{0:T(128)}, s32[10]{0:T(128)S(1)}, u32[]{:S(2)}) copy-start(s32[10]{0:T(128)S(1)} %pad_add_fusion.info_ref) | copy-start | bytes 124
  35.8 7.8 %collective-permute-start.5 = (bf16[512,384]{1,0:T(8,128)(2,1)}, bf16[512,384]{1,0:T(8,128)(2,1)S(1)}, u32[]{:S(2)}, u32[]{:S(2)}) collective-permute-start(bf16[512,384]{1,0:T(8,128)(2,1)} %collective-permute-done.4.f2), channel_id=1, source_target_pairs={{0,1},{1,0},{2,3},{3,2},{4,5},{5,4},{6,7},{7,6},{8,9},{9,8},{10,11... | collective-permute-start | bytes 1179656 | tf_op jit(solution)/shard_map/ppermute | solution.py:572
  35.8 4.2 %collective-permute-start.2 = (bf16[512,768]{1,0:T(8,128)(2,1)S(1)}, bf16[512,768]{1,0:T(8,128)(2,1)S(1)}, u32[]{:S(2)}, u32[]{:S(2)}) collective-permute-start(bf16[512,768]{1,0:T(8,128)(2,1)S(1)} %collective-permute-done.1), channel_id=1, source_target_pairs={{0,1},{1,0},{2,3},{3,2},{4,5},{5,4},{6,7},{7,6},{8,9},{9,8},{10,11... | collective-permute-start | bytes 2359304 | tf_op jit(solution)/shard_map/ppermute | solution.py:572
  37.1 54.1 %collective-permute-start.6 = (bf16[512,768]{1,0:T(8,128)(2,1)}, bf16[512,768]{1,0:T(8,128)(2,1)}, u32[]{:S(2)}, u32[]{:S(2)}) collective-permute-start(bf16[512,768]{1,0:T(8,128)(2,1)} %cot_ref.1), channel_id=1, source_target_pairs={{0,2},{1,3},{2,0},{3,1},{4,6},{5,7},{6,4},{7,5},{8,10},{9,11},{10,... | collective-permute-start | bytes 2359304 | tf_op jit(solution)/shard_map/ppermute | solution.py:568
  43.5 45.7 %copy-start = (bf16[512,768]{1,0:T(8,128)(2,1)}, bf16[512,768]{1,0:T(8,128)(2,1)S(1)}, u32[]{:S(2)}) copy-start(bf16[512,768]{1,0:T(8,128)(2,1)S(1)} %get-tuple-element.168.x3) | copy-start | bytes 2359300
  43.5 45.7 %copy-start.1 = (bf16[512,768]{1,0:T(8,128)(2,1)}, bf16[512,768]{1,0:T(8,128)(2,1)S(1)}, u32[]{:S(2)}) copy-start(bf16[512,768]{1,0:T(8,128)(2,1)S(1)} %get-tuple-element.169.x1) | copy-start | bytes 2359300
  43.5 45.7 %copy-start.2 = (bf16[512,768]{1,0:T(8,128)(2,1)}, bf16[512,768]{1,0:T(8,128)(2,1)S(1)}, u32[]{:S(2)}) copy-start(bf16[512,768]{1,0:T(8,128)(2,1)S(1)} %get-tuple-element.170.x2) | copy-start | bytes 2359300
  43.5 45.7 %copy-start.3 = (bf16[512,768]{1,0:T(8,128)(2,1)}, bf16[512,768]{1,0:T(8,128)(2,1)S(1)}, u32[]{:S(2)}) copy-start(bf16[512,768]{1,0:T(8,128)(2,1)S(1)} %get-tuple-element.171.x0) | copy-start | bytes 2359300
  62.0 52.2 %copy-start.35 = (f32[768]{0:T(1024)S(1)}, f32[768]{0:T(1024)}, u32[]{:S(2)}) copy-start(f32[768]{0:T(1024)} %param.24) | copy-start | bytes 9220
  91.2 15.0 %collective-permute-start.8 = (bf16[2,512,192]{2,1,0:T(8,128)(2,1)}, bf16[2,512,192]{2,1,0:T(8,128)(2,1)S(1)}, u32[]{:S(2)}, u32[]{:S(2)}) collective-permute-start(bf16[2,512,192]{2,1,0:T(8,128)(2,1)} %get-tuple-element.66.pair_ref), channel_id=1, source_target_pairs={{0,2},{1,3},{2,0},{3,1},{4,6},{5,7},{6,4},{7,5},{8,10},{9,11},{10,... | collective-permute-start | bytes 1179656 | tf_op jit(solution)/shard_map/ppermute | solution.py:568
  92.3 21.4 %collective-permute-start.11 = (bf16[768,192]{1,0:T(8,128)(2,1)S(1)}, bf16[768,192]{1,0:T(8,128)(2,1)S(1)}, u32[]{:S(2)}, u32[]{:S(2)}) collective-permute-start(bf16[768,192]{1,0:T(8,128)(2,1)S(1)} %slice.83.w0), channel_id=1, source_target_pairs={{0,2},{1,3},{2,0},{3,1},{4,6},{5,7},{6,4},{7,5},{8,10},{9,11},{10,... | collective-permute-start | bytes 884744 | tf_op jit(solution)/shard_map/ppermute | solution.py:568
  106.2 9.6 %collective-permute-start.9 = (bf16[2,512,192]{2,1,0:T(8,128)(2,1)S(1)}, bf16[2,512,192]{2,1,0:T(8,128)(2,1)S(1)}, u32[]{:S(2)}, u32[]{:S(2)}) collective-permute-start(bf16[2,512,192]{2,1,0:T(8,128)(2,1)S(1)} %collective-permute-done.8.h2), channel_id=1, source_target_pairs={{0,1},{1,0},{2,3},{3,2},{4,5},{5,4},{6,7},{7,6},{8,9},{9,8},{10,11... | collective-permute-start | bytes 1179656 | tf_op jit(solution)/shard_map/ppermute | solution.py:572
  106.2 9.6 %collective-permute-start.10 = (bf16[768,192]{1,0:T(8,128)(2,1)S(1)}, bf16[768,192]{1,0:T(8,128)(2,1)S(1)}, u32[]{:S(2)}, u32[]{:S(2)}) collective-permute-start(bf16[768,192]{1,0:T(8,128)(2,1)S(1)} %slice.83.w0), channel_id=1, source_target_pairs={{0,1},{1,0},{2,3},{3,2},{4,5},{5,4},{6,7},{7,6},{8,9},{9,8},{10,11... | collective-permute-start | bytes 884744 | tf_op jit(solution)/shard_map/ppermute | solution.py:572
  113.6 2.2 collective-permute-start.12
  113.6 2.2 collective-permute-start.7
  121.6 19.8 %collective-permute-start.16 = (bf16[512,768]{1,0:T(8,128)(2,1)}, bf16[512,768]{1,0:T(8,128)(2,1)S(1)}, u32[]{:S(2)}, u32[]{:S(2)}) collective-permute-start(bf16[512,768]{1,0:T(8,128)(2,1)} %get-tuple-element.68.x0), channel_id=1, source_target_pairs={{0,2},{1,3},{2,0},{3,1},{4,6},{5,7},{6,4},{7,5},{8,10},{9,11},{10,... | collective-permute-start | bytes 2359304 | tf_op jit(solution)/shard_map/ppermute | solution.py:568
  121.8 20.1 %collective-permute-start.18 = (bf16[512,768]{1,0:T(8,128)(2,1)}, bf16[512,768]{1,0:T(8,128)(2,1)S(1)}, u32[]{:S(2)}, u32[]{:S(2)}) collective-permute-start(bf16[512,768]{1,0:T(8,128)(2,1)} %collective-permute-done.6.c0.c2), channel_id=1, source_target_pairs={{0,1},{1,0},{2,3},{3,2},{4,5},{5,4},{6,7},{7,6},{8,9},{9,8},{10,11... | collective-permute-start | bytes 2359304 | tf_op jit(solution)/shard_map/ppermute | solution.py:572
  141.4 3.4 collective-permute-start.17
  141.4 13.5 %collective-permute-start.14 = (bf16[512,768]{1,0:T(8,128)(2,1)}, bf16[512,768]{1,0:T(8,128)(2,1)S(1)}, u32[]{:S(2)}, u32[]{:S(2)}) collective-permute-start(bf16[512,768]{1,0:T(8,128)(2,1)} %cot_ref.1), channel_id=1, source_target_pairs={{0,1},{1,0},{2,3},{3,2},{4,5},{5,4},{6,7},{7,6},{8,9},{9,8},{10,11... | collective-permute-start | bytes 2359304 | tf_op jit(solution)/shard_map/ppermute | solution.py:572
  141.9 13.0 %collective-permute-start.13 = (bf16[512,768]{1,0:T(8,128)(2,1)}, bf16[512,768]{1,0:T(8,128)(2,1)S(1)}, u32[]{:S(2)}, u32[]{:S(2)}) collective-permute-start(bf16[512,768]{1,0:T(8,128)(2,1)} %get-tuple-element.68.x0), channel_id=1, source_target_pairs={{0,1},{1,0},{2,3},{3,2},{4,5},{5,4},{6,7},{7,6},{8,9},{9,8},{10,11... | collective-permute-start | bytes 2359304 | tf_op jit(solution)/shard_map/ppermute | solution.py:572
  154.7 13.2 %collective-permute-start.21 = (bf16[512,768]{1,0:T(8,128)(2,1)}, bf16[512,768]{1,0:T(8,128)(2,1)S(1)}, u32[]{:S(2)}, u32[]{:S(2)}) collective-permute-start(bf16[512,768]{1,0:T(8,128)(2,1)} %get-tuple-element.80), channel_id=1, source_target_pairs={{0,1},{1,0},{2,3},{3,2},{4,5},{5,4},{6,7},{7,6},{8,9},{9,8},{10,11... | collective-permute-start | bytes 2359304 | tf_op jit(solution)/shard_map/ppermute | solution.py:572
  167.4 14.3 %collective-permute-start.20 = (bf16[512,768]{1,0:T(8,128)(2,1)}, bf16[512,768]{1,0:T(8,128)(2,1)S(1)}, u32[]{:S(2)}, u32[]{:S(2)}) collective-permute-start(bf16[512,768]{1,0:T(8,128)(2,1)} %get-tuple-element.78), channel_id=1, source_target_pairs={{0,1},{1,0},{2,3},{3,2},{4,5},{5,4},{6,7},{7,6},{8,9},{9,8},{10,11... | collective-permute-start | bytes 2359304 | tf_op jit(solution)/shard_map/ppermute | solution.py:572
  168.2 19.6 %collective-permute-start.22 = (bf16[512,768]{1,0:T(8,128)(2,1)S(1)}, bf16[512,768]{1,0:T(8,128)(2,1)S(1)}, u32[]{:S(2)}, u32[]{:S(2)}) collective-permute-start(bf16[512,768]{1,0:T(8,128)(2,1)S(1)} %add_convert_fusion.1), channel_id=1, source_target_pairs={{0,2},{1,3},{2,0},{3,1},{4,6},{5,7},{6,4},{7,5},{8,10},{9,11},{10,... | collective-permute-start | bytes 2359304 | tf_op jit(solution)/shard_map/ppermute | solution.py:568
  181.7 19.7 %collective-permute-start.19 = (bf16[512,768]{1,0:T(8,128)(2,1)}, bf16[512,768]{1,0:T(8,128)(2,1)S(1)}, u32[]{:S(2)}, u32[]{:S(2)}) collective-permute-start(bf16[512,768]{1,0:T(8,128)(2,1)} %get-tuple-element.76), channel_id=1, source_target_pairs={{0,1},{1,0},{2,3},{3,2},{4,5},{5,4},{6,7},{7,6},{8,9},{9,8},{10,11... | collective-permute-start | bytes 2359304 | tf_op jit(solution)/shard_map/ppermute | solution.py:572
  201.0 14.9 %collective-permute-start.27 = (bf16[2,768,192]{1,2,0:T(8,128)(2,1)}, bf16[2,768,192]{1,2,0:T(8,128)(2,1)}, u32[]{:S(2)}, u32[]{:S(2)}) collective-permute-start(bf16[2,768,192]{1,2,0:T(8,128)(2,1)} %copy.40), channel_id=1, source_target_pairs={{0,1},{1,0},{2,3},{3,2},{4,5},{5,4},{6,7},{7,6},{8,9},{9,8},{10,11... | collective-permute-start | bytes 1769480 | tf_op jit(solution)/shard_map/ppermute | solution.py:572
  201.0 14.7 %collective-permute-start.23 = (bf16[2,512,192]{2,1,0:T(8,128)(2,1)}, bf16[2,512,192]{2,1,0:T(8,128)(2,1)}, u32[]{:S(2)}, u32[]{:S(2)}) collective-permute-start(bf16[2,512,192]{2,1,0:T(8,128)(2,1)} %get-tuple-element.81), channel_id=1, source_target_pairs={{0,2},{1,3},{2,0},{3,1},{4,6},{5,7},{6,4},{7,5},{8,10},{9,11},{10,... | collective-permute-start | bytes 1179656 | tf_op jit(solution)/shard_map/ppermute | solution.py:568
  202.4 16.7 %collective-permute-start.25 = (bf16[512,192]{1,0:T(8,128)(2,1)}, bf16[512,192]{1,0:T(8,128)(2,1)}, u32[]{:S(2)}, u32[]{:S(2)}) collective-permute-start(bf16[512,192]{1,0:T(8,128)(2,1)} %get-tuple-element.87), channel_id=1, source_target_pairs={{0,1},{1,0},{2,3},{3,2},{4,5},{5,4},{6,7},{7,6},{8,9},{9,8},{10,11... | collective-permute-start | bytes 589832 | tf_op jit(solution)/shard_map/ppermute | solution.py:572
  215.7 37.3 %collective-permute-start.24 = (bf16[512,768]{1,0:T(8,128)(2,1)}, bf16[512,768]{1,0:T(8,128)(2,1)S(1)}, u32[]{:S(2)}, u32[]{:S(2)}) collective-permute-start(bf16[512,768]{1,0:T(8,128)(2,1)} %add_convert_fusion.2), channel_id=1, source_target_pairs={{0,2},{1,3},{2,0},{3,1},{4,6},{5,7},{6,4},{7,5},{8,10},{9,11},{10,... | collective-permute-start | bytes 2359304 | tf_op jit(solution)/shard_map/ppermute | solution.py:568
  216.0 3.2 collective-permute-start.26
  217.3 35.7 %collective-permute-start.28 = (bf16[768,192]{1,0:T(8,128)(2,1)S(1)}, bf16[768,192]{1,0:T(8,128)(2,1)S(1)}, u32[]{:S(2)}, u32[]{:S(2)}) collective-permute-start(bf16[768,192]{1,0:T(8,128)(2,1)S(1)} %fusion.21), channel_id=1, source_target_pairs={{0,2},{1,3},{2,0},{3,1},{4,6},{5,7},{6,4},{7,5},{8,10},{9,11},{10,... | collective-permute-start | bytes 884744 | tf_op jit(solution)/shard_map/ppermute | solution.py:568
  259.4 2.6 collective-permute-start.30
  259.8 7.0 %collective-permute-start.15 = (bf16[512,768]{1,0:T(8,128)(2,1)}, bf16[512,768]{1,0:T(8,128)(2,1)}, u32[]{:S(2)}, u32[]{:S(2)}) collective-permute-start(bf16[512,768]{1,0:T(8,128)(2,1)} %get-tuple-element.70), channel_id=1, source_target_pairs={{0,1},{1,0},{2,3},{3,2},{4,5},{5,4},{6,7},{7,6},{8,9},{9,8},{10,11... | collective-permute-start | bytes 2359304 | tf_op jit(solution)/shard_map/ppermute | solution.py:572
  260.0 13.3 %collective-permute-start.29 = (bf16[512,768]{1,0:T(8,128)(2,1)}, bf16[512,768]{1,0:T(8,128)(2,1)S(1)}, u32[]{:S(2)}, u32[]{:S(2)}) collective-permute-start(bf16[512,768]{1,0:T(8,128)(2,1)} %get-tuple-element.96), channel_id=1, source_target_pairs={{0,1},{1,0},{2,3},{3,2},{4,5},{5,4},{6,7},{7,6},{8,9},{9,8},{10,11... | collective-permute-start | bytes 2359304 | tf_op jit(solution)/shard_map/ppermute | solution.py:572
  264.2 20.1 %collective-permute-start.31 = (bf16[512,768]{1,0:T(8,128)(2,1)}, bf16[512,768]{1,0:T(8,128)(2,1)}, u32[]{:S(2)}, u32[]{:S(2)}) collective-permute-start(bf16[512,768]{1,0:T(8,128)(2,1)} %add_convert_fusion), channel_id=1, source_target_pairs={{0,2},{1,3},{2,0},{3,1},{4,6},{5,7},{6,4},{7,5},{8,10},{9,11},{10,... | collective-permute-start | bytes 2359304 | tf_op jit(solution)/shard_map/ppermute | solution.py:568
  293.3 12.2 %all-to-all-start.2 = ((f32[32,1,1540]{2,1,0:T(1,128)}), f32[32,1,1540]{2,1,0:T(1,128)S(1)}, u32[]{:S(2)}, u32[]{:S(2)}) async-start(f32[32,1,1540]{2,1,0:T(1,128)} %broadcast_in_dim.14), calls=%async_computation.3 | async-start | bytes 425984 | tf_op jit(solution)/shard_map/all_to_all | solution.py:704
  305.5 34.4 %all-to-all-start.1 = ((bf16[8,96,768]{2,1,0:T(8,128)(2,1)}), bf16[8,96,768]{2,1,0:T(8,128)(2,1)S(1)}, u32[]{:S(2)}, u32[]{:S(2)}) async-start(bf16[8,96,768]{2,1,0:T(8,128)(2,1)} %bitcast.8), calls=%async_computation.1 | async-start | bytes 2359296 | tf_op jit(solution)/shard_map/all_to_all | solution.py:676
  311.0 32.5 %collective-permute-start.32 = (bf16[2,512,192]{2,1,0:T(8,128)(2,1)S(1)}, bf16[2,512,192]{2,1,0:T(8,128)(2,1)S(1)}, u32[]{:S(2)}, u32[]{:S(2)}) collective-permute-start(bf16[2,512,192]{2,1,0:T(8,128)(2,1)S(1)} %copy-done.43), channel_id=1, source_target_pairs={{2,0},{3,1},{6,4},{7,5},{10,8},{11,9},{14,12},{15,13},{18,16},{19,... | collective-permute-start | bytes 1179656 | tf_op jit(solution)/shard_map/ppermute | solution.py:679
  315.8 27.7 %copy-start.32 = (bf16[512,192]{1,0:T(8,128)(2,1)S(1)}, bf16[512,192]{1,0:T(8,128)(2,1)}, u32[]{:S(2)}) copy-start(bf16[512,192]{1,0:T(8,128)(2,1)} %get-tuple-element.102) | copy-start | bytes 589828
  340.1 5.6 %collective-permute-start.34 = (f32[96,192]{1,0:T(8,128)S(1)}, f32[96,192]{1,0:T(8,128)S(1)}, u32[]{:S(2)}, u32[]{:S(2)}) collective-permute-start(f32[96,192]{1,0:T(8,128)S(1)} %slice.90), channel_id=1, source_target_pairs={{0,2},{1,3},{4,6},{5,7},{8,10},{9,11},{12,14},{13,15},{16,18},{17,... | collective-permute-start | bytes 221192 | tf_op jit(solution)/shard_map/ppermute | solution.py:691
  343.6 3.6 %collective-permute-start.33 = (bf16[512,192]{1,0:T(8,128)(2,1)S(1)}, bf16[512,192]{1,0:T(8,128)(2,1)S(1)}, u32[]{:S(2)}, u32[]{:S(2)}) collective-permute-start(bf16[512,192]{1,0:T(8,128)(2,1)S(1)} %get-tuple-element.161), channel_id=1, source_target_pairs={{0,1},{1,0},{2,3},{3,2},{4,5},{5,4},{6,7},{7,6},{8,9},{9,8},{10,11... | collective-permute-start | bytes 589832 | tf_op jit(solution)/shard_map/ppermute | solution.py:572
  346.4 1.9 collective-permute-start.35
  (37 other events, 217.3 us)
Sparse Core Ops, SparseCore 0:
  16.0 71.3 all-gather.1
  201.5 68.6 reduce-scatter.1
